TPU v7x, 32 devices: a whole 2x2x4 slice. The times are simulated.
32 devices in a mesh: dp: 2 (over y), ctx: 16 (over z, x, core).
Axes of the slice: x: 2, y: 2, z: 4, core: 2. Of those that a mesh axis runs over, the one named last changes fastest.
Arguments:
- tokens: bfloat16 [2, 2048, 2048], P('dp', 'ctx'), may hold values from -6 to 6
- cotangent: bfloat16 [2, 2048, 2048], P('dp', 'ctx'), may hold values from -6 to 6
- norm_gains: float32 [2, 2048], replicated, may hold values from 0.1 to 1.9
- head_gains: float32 [2, 64], replicated, may hold values from 1 to 2
- input_weight: float32 [2048, 2304], P(('dp', 'ctx')), may hold values from -0.125 to 0.125
- output_weight: float32 [1536, 2048], P(('dp', 'ctx')), may hold values from -1.25 to 1.25
- expand_weight: float32 [2048, 10240], P(('dp', 'ctx')), may hold values from -0.125 to 0.125
- reduce_weight: float32 [5120, 2048], P(('dp', 'ctx')), may hold values from -0.078125 to 0.078125
- norm_moment: float32 [2, 2048], replicated, may hold values from -6 to 6
- head_moment: float32 [2, 64], replicated, may hold values from -6 to 6
- input_moment: float32 [2048, 2304], P(('dp', 'ctx')), may hold values from -6 to 6
- output_moment: float32 [1536, 2048], P(('dp', 'ctx')), may hold values from -6 to 6
- expand_moment: float32 [2048, 10240], P(('dp', 'ctx')), may hold values from -6 to 6
- reduce_moment: float32 [5120, 2048], P(('dp', 'ctx')), may hold values from -6 to 6
- learn_rate: float32 [], replicated, may hold values from 0.05 to 0.2
Outputs:
- layer_out: bfloat16 [2, 2048, 2048], P('dp', 'ctx')
- token_grad: bfloat16 [2, 2048, 2048], P('dp', 'ctx')
- grad_norm: float32 [], replicated
- moment_norms: float32 [2, 2048], replicated
- moment_heads: float32 [2, 64], replicated
- moment_input: float32 [2048, 2304], P(('dp', 'ctx'))
- moment_output: float32 [1536, 2048], P(('dp', 'ctx'))
- moment_expand: float32 [2048, 10240], P(('dp', 'ctx'))
- moment_reduce: float32 [5120, 2048], P(('dp', 'ctx'))
- next_norms: float32 [2, 2048], replicated
- next_heads: float32 [2, 64], replicated
- next_input: float32 [2048, 2304], P(('dp', 'ctx'))
- next_output: float32 [1536, 2048], P(('dp', 'ctx'))
- next_expand: float32 [2048, 10240], P(('dp', 'ctx'))
- next_reduce: float32 [5120, 2048], P(('dp', 'ctx'))
All inputs are finite; a program needn't handle non-finite values.
Results may differ from a plain program's by a relative error of at most 0.03.
Values may be sent and summed in bfloat16 or wider, within the bound.
A program may use at most 320 MiB of HBM per device.

v0:
```python
import math

import jax
import jax.numpy as jnp
from jax import lax
from jax.sharding import PartitionSpec as P

HEADS = 24
KV_HEADS = 6
HD = 64
FF = 5120
GROUP = 4
NPARAM = 39325824


EPSILON = 1e-06
THETA = 10000.0
NEGATIVE = -1e30
MOMENTUM = 0.5


def rms_normed(values, gains):
    mean_square = jnp.mean(values * values, axis=-1, keepdims=True)
    return values * lax.rsqrt(mean_square + EPSILON) * gains


def rotary(values, positions):
    half_width = values.shape[-1] // 2
    frequency = THETA ** (-2.0 * jnp.arange(half_width).astype(jnp.float32) / values.shape[-1])
    angles = positions.astype(jnp.float32)[:, None] * frequency[None, :]
    cosine = jnp.cos(angles)[:, None, :]
    sine_rows = jnp.sin(angles)[:, None, :]
    front_half = values[..., :half_width]
    back_half = values[..., half_width:]
    return jnp.concatenate(
        [front_half * cosine - back_half * sine_rows, back_half * cosine + front_half * sine_rows],
        axis=-1,
    )


def prepare(projected, head_gains, positions):
    row_count = projected.shape[0]
    queries = projected[:, : HEADS * HD].reshape(row_count, HEADS, HD)
    key_rows = projected[:, HEADS * HD : (HEADS + KV_HEADS) * HD].reshape(row_count, KV_HEADS, HD)
    value_rows = projected[:, (HEADS + KV_HEADS) * HD :].reshape(row_count, KV_HEADS, HD)
    queries = rotary(rms_normed(queries, head_gains[0]), positions)
    key_rows = rotary(rms_normed(key_rows, head_gains[1]), positions)
    return (queries, key_rows, value_rows)


def place_of(device, row_index, rows_dev):
    return device * rows_dev + row_index


def on_device(
    tokens,
    cotangent,
    norm_gains,
    head_gains,
    input_weight,
    output_weight,
    expand_weight,
    reduce_weight,
    norm_moment,
    head_moment,
    input_moment,
    output_moment,
    expand_moment,
    reduce_moment,
    learn_rate,
):
    seq_count, rows_dev, model_width = tokens.shape
    cycle_size = lax.axis_size("ctx")
    cycle_index = lax.axis_index("ctx")
    token_rows, upstream = (tokens, cotangent)
    total_rows = seq_count * rows_dev
    half_rows = rows_dev // 2
    kv_width = KV_HEADS * HD
    score_scale = 1.0 / math.sqrt(HD)
    row_index = jnp.arange(rows_dev, dtype=jnp.int32)
    query_place = place_of(cycle_index, row_index, rows_dev)
    positions = jnp.tile(query_place, seq_count)
    full_input, full_output, full_expand, full_reduce = (
        lax.all_gather(input_weight.astype(jnp.bfloat16), ("dp", "ctx"), axis=0, tiled=True),
        lax.all_gather(output_weight.astype(jnp.bfloat16), ("dp", "ctx"), axis=0, tiled=True),
        lax.all_gather(expand_weight.astype(jnp.bfloat16), ("dp", "ctx"), axis=0, tiled=True),
        lax.all_gather(reduce_weight.astype(jnp.bfloat16), ("dp", "ctx"), axis=0, tiled=True),
    )
    input_rows = token_rows.reshape(total_rows, model_width).astype(jnp.float32)
    normed_one, norm_one_pull = jax.vjp(rms_normed, input_rows, norm_gains[0])
    normed_one = normed_one.astype(jnp.bfloat16)
    projected = jnp.dot(normed_one, full_input, preferred_element_type=jnp.float32)

    def prepare_here(projected_rows, gains):
        return prepare(projected_rows, gains, positions)

    prepared, prepare_pull = jax.vjp(prepare_here, projected, head_gains)
    queries, key_rows, value_rows = prepared
    query_low = queries.astype(jnp.bfloat16).reshape(seq_count, rows_dev, KV_HEADS, GROUP, HD)
    kv_low = jnp.concatenate(
        [key_rows.reshape(total_rows, kv_width), value_rows.reshape(total_rows, kv_width)], axis=1
    )
    kv_low = kv_low.astype(jnp.bfloat16).reshape(seq_count, rows_dev, 2 * kv_width)

    def split_pair(kv_part):
        key_part = kv_part[:, :, :kv_width].reshape(seq_count, -1, KV_HEADS, HD)
        value_part = kv_part[:, :, kv_width:].reshape(seq_count, -1, KV_HEADS, HD)
        return (key_part, value_part)

    def fold_update(state, query_part, query_pos, kv_part, key_pos):
        running_max, running_sum, running_out = state
        key_part, value_part = split_pair(kv_part)
        scores = (
            jnp.einsum(
                "sqkgd,snkd->skgqn", query_part, key_part, preferred_element_type=jnp.float32
            )
            * score_scale
        )
        allowed = key_pos[None, :] <= query_pos[:, None]
        masked = jnp.where(allowed, scores, NEGATIVE)
        new_max = jnp.maximum(running_max, jnp.max(masked, axis=-1))
        weights = jnp.where(allowed, jnp.exp(masked - new_max[..., None]), 0.0)
        rescale = jnp.exp(running_max - new_max)
        new_sum = rescale * running_sum + jnp.sum(weights, axis=-1)
        new_out = rescale[..., None] * running_out + jnp.einsum(
            "skgqn,snkd->skgqd",
            weights.astype(jnp.bfloat16),
            value_part,
            preferred_element_type=jnp.float32,
        )
        return (new_max, new_sum, new_out)

    def visit_forward(states, kv_part, key_pos, source):

        def compute(current):
            return (
                fold_update(
                    current[0], query_low[:, :half_rows], query_place[:half_rows], kv_part, key_pos
                ),
                fold_update(
                    current[1], query_low[:, half_rows:], query_place[half_rows:], kv_part, key_pos
                ),
            )

        def unchanged(current):
            return current

        return lax.cond(source <= cycle_index, compute, unchanged, states)

    def empty_state():
        return (
            jnp.full((seq_count, KV_HEADS, GROUP, half_rows), NEGATIVE, jnp.float32),
            jnp.zeros((seq_count, KV_HEADS, GROUP, half_rows), jnp.float32),
            jnp.zeros((seq_count, KV_HEADS, GROUP, half_rows, HD), jnp.float32),
        )

    kv_piece = lax.all_gather(kv_low, "ctx", axis=1, tiled=True)

    def fold_one_block(block_turn, current):
        kv_part = lax.dynamic_slice_in_dim(kv_piece, block_turn * rows_dev, rows_dev, 1)
        key_pos = place_of(block_turn, row_index, rows_dev)
        return visit_forward(current, kv_part, key_pos, block_turn)

    lower_half, upper_half = lax.fori_loop(
        0, kv_piece.shape[1] // rows_dev, fold_one_block, (empty_state(), empty_state())
    )
    running_max = jnp.concatenate([lower_half[0], upper_half[0]], axis=-1)
    running_sum = jnp.concatenate([lower_half[1], upper_half[1]], axis=-1)
    running_out = jnp.concatenate([lower_half[2], upper_half[2]], axis=-2)
    attended = running_out / running_sum[..., None]
    log_mass = running_max + jnp.log(running_sum)
    attended_low = (
        attended.transpose(0, 3, 1, 2, 4).reshape(total_rows, HEADS * HD).astype(jnp.bfloat16)
    )
    branch = jnp.dot(attended_low, full_output, preferred_element_type=jnp.float32)
    residual = input_rows + branch
    normed_two, norm_two_pull = jax.vjp(rms_normed, residual, norm_gains[1])
    normed_two = normed_two.astype(jnp.bfloat16)
    expanded = jnp.dot(normed_two, full_expand, preferred_element_type=jnp.float32)
    gate_value = expanded[:, :FF]
    up_value = expanded[:, FF:]
    sigmoid = jax.nn.sigmoid(gate_value)
    activated = gate_value * sigmoid
    slope = sigmoid * (1.0 + gate_value * (1.0 - sigmoid))
    hidden = (activated * up_value).astype(jnp.bfloat16)
    result = residual + jnp.dot(hidden, full_reduce, preferred_element_type=jnp.float32)
    result_low = result.astype(jnp.bfloat16).reshape(seq_count, rows_dev, model_width)
    upstream_low = upstream.reshape(total_rows, model_width)
    grad_reduce = jnp.einsum("rf,rd->fd", hidden, upstream_low, preferred_element_type=jnp.float32)
    hidden_grad = jnp.einsum(
        "rd,fd->rf", upstream_low, full_reduce, preferred_element_type=jnp.float32
    )
    expand_grad = jnp.concatenate(
        [hidden_grad * up_value * slope, hidden_grad * activated], axis=1
    ).astype(jnp.bfloat16)
    grad_expand = jnp.einsum(
        "rd,rf->df", normed_two, expand_grad, preferred_element_type=jnp.float32
    )
    normed_two_grad = jnp.einsum(
        "rf,df->rd", expand_grad, full_expand, preferred_element_type=jnp.float32
    )
    residual_part, gain_two_grad = norm_two_pull(normed_two_grad)
    residual_grad = upstream_low.astype(jnp.float32) + residual_part
    branch_grad = residual_grad.astype(jnp.bfloat16)
    grad_output = jnp.einsum(
        "rh,rd->hd", attended_low, branch_grad, preferred_element_type=jnp.float32
    )
    attended_grad = jnp.einsum(
        "rd,hd->rh", branch_grad, full_output, preferred_element_type=jnp.float32
    ).astype(jnp.bfloat16)
    grad_grouped = attended_grad.reshape(seq_count, rows_dev, KV_HEADS, GROUP, HD)
    row_delta = jnp.sum(
        grad_grouped.transpose(0, 2, 3, 1, 4).astype(jnp.float32) * attended, axis=-1
    )

    def block_grads(query_part, dout_part, mass_part, delta_part, query_pos, kv_part, key_pos):
        key_part, value_part = split_pair(kv_part)
        scores = (
            jnp.einsum(
                "sqkgd,snkd->skgqn", query_part, key_part, preferred_element_type=jnp.float32
            )
            * score_scale
        )
        allowed = key_pos[None, :] <= query_pos[:, None]
        prob_rows = jnp.where(allowed, jnp.exp(scores - mass_part[..., None]), 0.0)
        prob_grad = jnp.einsum(
            "sqkgd,snkd->skgqn", dout_part, value_part, preferred_element_type=jnp.float32
        )
        score_grad = (prob_rows * (prob_grad - delta_part[..., None])).astype(jnp.bfloat16)
        query_add = (
            jnp.einsum(
                "skgqn,snkd->sqkgd", score_grad, key_part, preferred_element_type=jnp.float32
            )
            * score_scale
        )
        key_add = (
            jnp.einsum(
                "skgqn,sqkgd->snkd", score_grad, query_part, preferred_element_type=jnp.float32
            )
            * score_scale
        )
        value_add = jnp.einsum(
            "skgqn,sqkgd->snkd",
            prob_rows.astype(jnp.bfloat16),
            dout_part,
            preferred_element_type=jnp.float32,
        )
        key_count = kv_part.shape[1]
        return (
            query_add,
            jnp.concatenate(
                [
                    key_add.reshape(seq_count, key_count, kv_width),
                    value_add.reshape(seq_count, key_count, kv_width),
                ],
                axis=2,
            ),
        )

    def pair_grads(kv_part, key_pos):
        return block_grads(
            query_low, grad_grouped, log_mass, row_delta, query_place, kv_part, key_pos
        )

    def skipped(kv_unused, pos_unused):
        return (
            jnp.zeros((seq_count, rows_dev, KV_HEADS, GROUP, HD), jnp.float32),
            jnp.zeros((seq_count, rows_dev, 2 * kv_width), jnp.float32),
        )

    back_start = (
        jnp.zeros((seq_count, rows_dev, KV_HEADS, GROUP, HD), jnp.float32),
        jnp.zeros((seq_count, rows_dev * cycle_size, 2 * kv_width), jnp.float32),
    )
    back_kv_piece = lax.all_gather(kv_low, "ctx", axis=1, tiled=True)

    def back_one_block(block_turn, current):
        query_grads, pair_totals = current
        kv_part = lax.dynamic_slice_in_dim(back_kv_piece, block_turn * rows_dev, rows_dev, 1)
        key_pos = place_of(block_turn, row_index, rows_dev)
        query_add, pair_add = lax.cond(
            block_turn <= cycle_index, pair_grads, skipped, kv_part, key_pos
        )
        stored = lax.dynamic_slice_in_dim(pair_totals, block_turn * rows_dev, rows_dev, 1)
        pair_totals = lax.dynamic_update_slice_in_dim(
            pair_totals, stored + pair_add, block_turn * rows_dev, 1
        )
        return (query_grads + query_add, pair_totals)

    query_grads, pair_totals = lax.fori_loop(
        0, back_kv_piece.shape[1] // rows_dev, back_one_block, back_start
    )
    pair_mine = lax.psum_scatter(pair_totals, "ctx", scatter_dimension=1, tiled=True)
    pair_flat = pair_mine.reshape(total_rows, 2 * kv_width)
    projected_grad, head_grads = prepare_pull(
        (
            query_grads.reshape(total_rows, HEADS, HD),
            pair_flat[:, :kv_width].reshape(total_rows, KV_HEADS, HD),
            pair_flat[:, kv_width:].reshape(total_rows, KV_HEADS, HD),
        )
    )
    projected_low = projected_grad.astype(jnp.bfloat16)
    grad_input = jnp.einsum(
        "rd,rc->dc", normed_one, projected_low, preferred_element_type=jnp.float32
    )
    normed_one_grad = jnp.einsum(
        "rc,dc->rd", projected_low, full_input, preferred_element_type=jnp.float32
    )
    input_part, gain_one_grad = norm_one_pull(normed_one_grad)
    token_low = (
        (residual_grad + input_part).astype(jnp.bfloat16).reshape(seq_count, rows_dev, model_width)
    )
    shard_input, shard_output, shard_expand, shard_reduce = (
        lax.psum_scatter(grad_input, ("dp", "ctx"), scatter_dimension=0, tiled=True),
        lax.psum_scatter(grad_output, ("dp", "ctx"), scatter_dimension=0, tiled=True),
        lax.psum_scatter(grad_expand, ("dp", "ctx"), scatter_dimension=0, tiled=True),
        lax.psum_scatter(grad_reduce, ("dp", "ctx"), scatter_dimension=0, tiled=True),
    )
    layer_out, token_grad = (result_low, token_low)
    squares_local = (
        jnp.sum(shard_input * shard_input)
        + jnp.sum(shard_output * shard_output)
        + jnp.sum(shard_expand * shard_expand)
        + jnp.sum(shard_reduce * shard_reduce)
    )
    gain_totals, head_totals, square_total = lax.psum(
        (jnp.stack([gain_one_grad, gain_two_grad]), head_grads, squares_local), ("dp", "ctx")
    )
    grad_norm = jnp.sqrt(
        square_total + jnp.sum(gain_totals * gain_totals) + jnp.sum(head_totals * head_totals)
    )
    clip_limit = math.sqrt(NPARAM)
    factor = clip_limit / jnp.maximum(grad_norm, clip_limit)

    def advance(weight, moment, gradient):
        new_moment = MOMENTUM * moment + factor * gradient
        return (new_moment, weight - learn_rate * new_moment)

    moment_norms, next_norms = advance(norm_gains, norm_moment, gain_totals)
    moment_heads, next_heads = advance(head_gains, head_moment, head_totals)
    moment_input, next_input = advance(input_weight, input_moment, shard_input)
    moment_output, next_output = advance(output_weight, output_moment, shard_output)
    moment_expand, next_expand = advance(expand_weight, expand_moment, shard_expand)
    moment_reduce, next_reduce = advance(reduce_weight, reduce_moment, shard_reduce)
    return (
        layer_out,
        token_grad,
        grad_norm,
        moment_norms,
        moment_heads,
        moment_input,
        moment_output,
        moment_expand,
        moment_reduce,
        next_norms,
        next_heads,
        next_input,
        next_output,
        next_expand,
        next_reduce,
    )


def solution(mesh):
    in_specs = (
        P("dp", "ctx", None),
        P("dp", "ctx", None),
        P(),
        P(),
        P(("dp", "ctx"), None),
        P(("dp", "ctx"), None),
        P(("dp", "ctx"), None),
        P(("dp", "ctx"), None),
        P(),
        P(),
        P(("dp", "ctx"), None),
        P(("dp", "ctx"), None),
        P(("dp", "ctx"), None),
        P(("dp", "ctx"), None),
        P(),
    )
    out_specs = (
        P("dp", "ctx", None),
        P("dp", "ctx", None),
        P(),
        P(),
        P(),
        P(("dp", "ctx"), None),
        P(("dp", "ctx"), None),
        P(("dp", "ctx"), None),
        P(("dp", "ctx"), None),
        P(),
        P(),
        P(("dp", "ctx"), None),
        P(("dp", "ctx"), None),
        P(("dp", "ctx"), None),
        P(("dp", "ctx"), None),
    )
    return jax.shard_map(
        on_device, mesh=mesh, in_specs=in_specs, out_specs=out_specs, check_vma=False
    )
```

profile of v0, /device:TPU:0, one launch (start us, length us, event | category | flops | bytes accessed | tf_op | source)
XLA Modules:
  0.0 2581.5 jit_solution(3357718965123608761)
XLA Ops:
  12.1 84.1 %all-gather.6.cloned.1.call-done = bf16[2048,2304]{1,0:T(8,128)(2,1)} async-done(((bf16[64,2304]{1,0:T(8,128)(2,1)}), bf16[2048,2304]{1,0:T(8,128)(2,1)}) %all-gather.6.cloned.1.call-update) | async-done | bytes 9437200 | tf_op jit(solution)/shard_map/all_gather | solution.py:84
  96.2 5.3 fusion.75
  111.5 37.9 %all-gather.8.cloned.1.call-done = bf16[1,2048,768]{2,1,0:T(8,128)(2,1)} async-done(((bf16[1,128,768]{2,1,0:T(8,128)(2,1)}), bf16[1,2048,768]{2,1,0:T(8,128)(2,1)}) %all-gather.8.cloned.1.call-update) | async-done | bytes 3145744 | tf_op jit(solution)/shard_map/all_gather | solution.py:157
  149.4 4.7 copy.52
  154.3 5.5 while.40
  154.3 4.6 conditional.6
  162.2 59.0 %all-gather.10.cloned.1.call-done = bf16[1536,2048]{1,0:T(8,128)(2,1)} async-done(((bf16[48,2048]{1,0:T(8,128)(2,1)}), bf16[1536,2048]{1,0:T(8,128)(2,1)}) %all-gather.10.cloned.1.call-update) | async-done | bytes 6291472 | tf_op jit(solution)/shard_map/all_gather | solution.py:85
  221.2 4.0 multiply_reduce_fusion.4
  225.3 233.0 %all-gather.12.cloned.1.call-done = bf16[2048,10240]{1,0:T(8,128)(2,1)} async-done(((bf16[64,10240]{1,0:T(8,128)(2,1)}), bf16[2048,10240]{1,0:T(8,128)(2,1)}) %all-gather.12.cloned.1.call-update) | async-done | bytes 41943056 | tf_op jit(solution)/shard_map/all_gather | solution.py:86
  458.3 18.9 fusion.86
  477.2 117.1 %all-gather.14.cloned.1.call-done = bf16[5120,2048]{1,0:T(8,128)(2,1)} async-done(((bf16[160,2048]{1,0:T(8,128)(2,1)}), bf16[5120,2048]{1,0:T(8,128)(2,1)}) %all-gather.14.cloned.1.call-update) | async-done | bytes 20971536 | tf_op jit(solution)/shard_map/all_gather | solution.py:87
  594.3 13.5 multiply_convert_fusion.1
  607.8 21.9 multiply_reduce_fusion.2
  633.4 3.0 convolution_convert_fusion
  639.3 3.4 broadcast_in_dim.83
  642.7 38.9 %while.41 = (s32[]{:T(128)}, f32[1,128,6,4,64]{1,4,3,2,0:T(8,128)S(1)}, f32[1,2048,768]{1,2,0:T(8,128)}, s32[]{:T(128)}, bf16[1,2048,768]{1,2,0:T(8,128)(2,1)}, ...) while((s32[]{:T(128)}, ...), condition=%wide.region_17.18_spmd.clone, body=%wide.region_14.17_spmd.clone.sunk | while | flops 255262976 | bytes 14905679 | solution.py:290
  642.7 3.1 conditional.7
  683.0 6.3 fusion.70
  691.5 117.7 %reduce-scatter.6.cloned.1.call-done = f32[1,128,768]{1,2,0:T(8,128)} async-done(((f32[1,2048,768]{1,2,0:T(8,128)}), f32[1,128,768]{1,2,0:T(8,128)}) %reduce-scatter.6.cloned.1.call-update) | async-done | bytes 393232 | tf_op jit(solution)/shard_map/reduce_scatter | solution.py:293
  812.6 8.0 fusion.73
  821.7 20.2 fusion.66
  843.2 33.8 %fusion.53 = f32[2048,10240]{1,0:T(8,128)} fusion(bf16[128,5120]{1,0:T(8,128)(2,1)} %get-tuple-element.799, bf16[128,5120]{1,0:T(8,128)(2,1)} %get-tuple-element.798, f32[128,2048]{1,0:T(8,128)S(1)} %copy-done.1, f32[2048]{0:T(1024)S(1)} %bitcast.244, f32[128]{0:T(128)S(1)} %fusion.82), kind=kOutput, calls=%fused_computation.92 | convolution fusion | flops 5374738432 | bytes 87564800 | tf_op jit(solution)/shard_map/rd,rf->df/dot_general | solution.py:196
  877.7 11.2 fusion.52
  889.0 7.2 fusion.58
  896.3 74.5 %reduce-scatter.10.cloned.1.call-done = f32[48,2048]{1,0:T(8,128)} async-done(((f32[1536,2048]{1,0:T(8,128)}), f32[48,2048]{1,0:T(8,128)}) %reduce-scatter.10.cloned.1.call-update) | async-done | bytes 393232 | tf_op jit(solution)/shard_map/reduce_scatter | solution.py:315
  972.4 210.6 %reduce-scatter.8.cloned.1.call-done = f32[64,2304]{1,0:T(8,128)} async-done(((f32[2048,2304]{1,0:T(8,128)}), f32[64,2304]{1,0:T(8,128)}) %reduce-scatter.8.cloned.1.call-update) | async-done | bytes 589840 | tf_op jit(solution)/shard_map/reduce_scatter | solution.py:314
  1186.2 438.3 %reduce-scatter.14.cloned.1.call-done = f32[160,2048]{1,0:T(8,128)} async-done(((f32[5120,2048]{1,0:T(8,128)}), f32[160,2048]{1,0:T(8,128)}) %reduce-scatter.14.cloned.1.call-update) | async-done | bytes 1310736 | tf_op jit(solution)/shard_map/reduce_scatter | solution.py:317
  1626.7 879.7 %reduce-scatter.12.cloned.1.call-done = f32[64,10240]{1,0:T(8,128)} async-done(((f32[2048,10240]{1,0:T(8,128)}), f32[64,10240]{1,0:T(8,128)}) %reduce-scatter.12.cloned.1.call-update) | async-done | bytes 2621456 | tf_op jit(solution)/shard_map/reduce_scatter | solution.py:316
  2506.4 3.0 multiply_reduce_fusion
  2511.9 44.9 %all-reduce.9 = (f32[]{:T(128)}, f32[2,2048]{1,0:T(2,128)S(1)}, f32[2,64]{1,0:T(2,128)S(1)}) all-reduce(f32[]{:T(128)S(6)} %add.300, f32[2,2048]{1,0:T(2,128)S(1)} %pad_maximum_fusion.7, f32[2,64]{1,0:T(2,128)S(1)} %pad_add_fusion.2), channel_id=1, replica_groups=mesh['dp'=2,'ctx'=16] {'dp','ctx'}, use_global_device_ids=true, to_apply=%region_30.31 | all-reduce | flops 4225 | bytes 33800 | tf_op jit(solution)/shard_map/psum | solution.py:326
  2561.3 2.5 multiply_subtract_fusion.2
  2565.9 5.6 multiply_subtract_fusion
  (346 shorter events, 90.9 us)
Async XLA Ops:
  7.2 89.0 %all-gather.6.cloned.1.call-start = ((), (), s32[]{:S(2)}) async-start(), calls=%async_computation.5 | async-start | bytes 9732096 | tf_op jit(solution)/shard_map/all_gather | solution.py:84
  9.1 140.3 %all-gather.8.cloned.1.call-start = ((), (), s32[]{:S(2)}) async-start(), calls=%async_computation.6 | async-start | bytes 3342336 | tf_op jit(solution)/shard_map/all_gather | solution.py:157
  10.4 91.2 %copy-start.39 = (f32[128]{0:T(128)}, f32[128]{0:T(128)S(1)}, u32[]{:S(2)}) copy-start(f32[128]{0:T(128)S(1)} %fusion.81) | copy-start | bytes 1540
  11.2 91.7 %copy-start.43 = (f32[64]{0:T(128)}, f32[64]{0:T(128)S(1)}, u32[]{:S(2)}) copy-start(f32[64]{0:T(128)S(1)} %get-tuple-element.816) | copy-start | bytes 772
  11.2 99.1 %copy-start.44 = (f32[64]{0:T(128)}, f32[64]{0:T(128)S(1)}, u32[]{:S(2)}) copy-start(f32[64]{0:T(128)S(1)} %get-tuple-element.815) | copy-start | bytes 772
  11.3 99.2 %copy-start.28 = (f32[128,32]{0,1:T(8,128)}, f32[128,32]{0,1:T(8,128)S(1)}, u32[]{:S(2)}) copy-start(f32[128,32]{0,1:T(8,128)S(1)} %get-tuple-element.818) | copy-start | bytes 49156
  105.2 116.0 %all-gather.10.cloned.1.call-start = ((), (), s32[]{:S(2)}) async-start(), calls=%async_computation.7 | async-start | bytes 6488064 | tf_op jit(solution)/shard_map/all_gather | solution.py:85
  106.0 352.3 %all-gather.12.cloned.1.call-start = ((), (), s32[]{:S(2)}) async-start(), calls=%async_computation.8 | async-start | bytes 43253760 | tf_op jit(solution)/shard_map/all_gather | solution.py:86
  107.3 487.0 %all-gather.14.cloned.1.call-start = ((), (), s32[]{:S(2)}) async-start(), calls=%async_computation.9 | async-start | bytes 21626880 | tf_op jit(solution)/shard_map/all_gather | solution.py:87
  109.6 699.5 %reduce-scatter.6.cloned.1.call-start = ((), (), s32[]{:S(2)}) async-start(), calls=%async_computation.10 | async-start | bytes 6684672 | tf_op jit(solution)/shard_map/reduce_scatter | solution.py:293
  159.8 61.4 %copy-start.3 = (bf16[1,128,2048]{2,1,0:T(8,128)(2,1)S(1)}, bf16[1,128,2048]{2,1,0:T(8,128)(2,1)}, u32[]{:S(2)}) copy-start(bf16[1,128,2048]{2,1,0:T(8,128)(2,1)} %param.23) | copy-start | bytes 1572868
  160.1 65.2 %copy-start.11 = (f32[1,6,4,64,64]{3,4,2,1,0:T(8,128)}, f32[1,6,4,64,64]{3,4,2,1,0:T(8,128)S(1)}, u32[]{:S(2)}) copy-start(f32[1,6,4,64,64]{3,4,2,1,0:T(8,128)S(1)} %copy.55) | copy-start | bytes 1179652
  160.4 60.9 %copy-start.12 = (f32[1,6,4,64,64]{3,4,2,1,0:T(8,128)}, f32[1,6,4,64,64]{3,4,2,1,0:T(8,128)S(1)}, u32[]{:S(2)}) copy-start(f32[1,6,4,64,64]{3,4,2,1,0:T(8,128)S(1)} %copy.54) | copy-start | bytes 1179652
  161.2 64.1 %copy-start.32 = (f32[6,4,128]{2,1,0:T(4,128)}, f32[6,4,128]{2,1,0:T(4,128)S(1)}, u32[]{:S(2)}) copy-start(f32[6,4,128]{2,1,0:T(4,128)S(1)} %get-tuple-element.812) | copy-start | bytes 36868
  225.3 251.9 %copy-start = (f32[128,2048]{1,0:T(8,128)}, f32[128,2048]{1,0:T(8,128)S(1)}, u32[]{:S(2)}) copy-start(f32[128,2048]{1,0:T(8,128)S(1)} %get-tuple-element.820) | copy-start | bytes 3145732
  225.3 251.9 %copy-start.51 = (f32[128]{0:T(128)}, f32[128]{0:T(128)S(1)}, u32[]{:S(2)}) copy-start(f32[128]{0:T(128)S(1)} %get-tuple-element.819) | copy-start | bytes 1540
  458.3 136.0 %copy-start.19 = (bf16[1,128,2048]{2,1,0:T(8,128)(2,1)S(1)}, bf16[1,128,2048]{2,1,0:T(8,128)(2,1)}, u32[]{:S(2)}) copy-start(bf16[1,128,2048]{2,1,0:T(8,128)(2,1)} %param.24) | copy-start | bytes 1572868
  607.8 25.6 slice-start.1
  681.7 289.1 %reduce-scatter.10.cloned.1.call-start = ((), (), s32[]{:S(2)}) async-start(), calls=%async_computation.12 | async-start | bytes 12976128 | tf_op jit(solution)/shard_map/reduce_scatter | solution.py:315
  689.4 493.7 %reduce-scatter.8.cloned.1.call-start = ((), (), s32[]{:S(2)}) async-start(), calls=%async_computation.11 | async-start | bytes 19464192 | tf_op jit(solution)/shard_map/reduce_scatter | solution.py:314
  690.5 119.8 %copy-start.17 = (f32[128,384]{0,1:T(8,128)S(1)}, f32[128,384]{0,1:T(8,128)}, u32[]{:S(2)}) copy-start(f32[128,384]{0,1:T(8,128)} %copy-done.16) | copy-start | bytes 589828
  690.5 120.6 %copy-start.37 = (f32[128,6]{0,1:T(8,128)S(1)}, f32[128,6]{0,1:T(8,128)}, u32[]{:S(2)}) copy-start(f32[128,6]{0,1:T(8,128)} %copy-done.36) | copy-start | bytes 9220
  691.2 121.3 %copy-start.4 = (bf16[1,128,2048]{2,1,0:T(8,128)(2,1)S(1)}, bf16[1,128,2048]{2,1,0:T(8,128)(2,1)}, u32[]{:S(2)}) copy-start(bf16[1,128,2048]{2,1,0:T(8,128)(2,1)} %param.23) | copy-start | bytes 1572868
  691.2 121.3 %copy-start.40 = (f32[128]{0:T(128)S(1)}, f32[128]{0:T(128)}, u32[]{:S(2)}) copy-start(f32[128]{0:T(128)} %copy-done.39) | copy-start | bytes 1540
  820.6 803.8 %reduce-scatter.14.cloned.1.call-start = ((), (), s32[]{:S(2)}) async-start(), calls=%async_computation.14 | async-start | bytes 43253760 | tf_op jit(solution)/shard_map/reduce_scatter | solution.py:317
  841.9 1664.5 %reduce-scatter.12.cloned.1.call-start = ((), (), s32[]{:S(2)}) async-start(), calls=%async_computation.13 | async-start | bytes 86507520 | tf_op jit(solution)/shard_map/reduce_scatter | solution.py:316
  1626.7 933.3 %copy-start.35 = (f32[2,2048]{1,0:T(2,128)S(1)}, f32[2,2048]{1,0:T(2,128)}, u32[]{:S(2)}) copy-start(f32[2,2048]{1,0:T(2,128)} %param.25) | copy-start | bytes 49156
  1626.7 933.4 %copy-start.41 = (f32[2,2048]{1,0:T(2,128)S(1)}, f32[2,2048]{1,0:T(2,128)}, u32[]{:S(2)}) copy-start(f32[2,2048]{1,0:T(2,128)} %param.31) | copy-start | bytes 49156
  1626.7 934.0 %copy-start.46 = (f32[2,64]{1,0:T(2,128)S(1)}, f32[2,64]{1,0:T(2,128)}, u32[]{:S(2)}) copy-start(f32[2,64]{1,0:T(2,128)} %param.26) | copy-start | bytes 1540
  1626.7 934.0 %copy-start.48 = (f32[2,64]{1,0:T(2,128)S(1)}, f32[2,64]{1,0:T(2,128)}, u32[]{:S(2)}) copy-start(f32[2,64]{1,0:T(2,128)} %param.32) | copy-start | bytes 1540
  2511.9 51.9 %copy-start.26 = (f32[48,2048]{1,0:T(8,128)S(1)}, f32[48,2048]{1,0:T(8,128)}, u32[]{:S(2)}) copy-start(f32[48,2048]{1,0:T(8,128)} %param.28) | copy-start | bytes 1179652
  2511.9 54.0 %copy-start.9 = (f32[64,10240]{1,0:T(8,128)S(1)}, f32[64,10240]{1,0:T(8,128)}, u32[]{:S(2)}) copy-start(f32[64,10240]{1,0:T(8,128)} %reduce-scatter.12.cloned.1.call-done) | copy-start | bytes 7864324
  (33 other events, 137.5 us)
Sparse Core Ops, SparseCore 0:
  11.5 84.7 all-gather.5
  105.3 43.9 all-gather.7
  152.8 68.3 all-gather.9
  224.6 233.6 all-gather.11
  461.6 132.6 all-gather.13
  681.8 127.3 reduce-scatter.5
  816.2 154.4 reduce-scatter.9
  977.1 205.8 reduce-scatter.7
  1185.4 439.0 reduce-scatter.13
  1626.7 879.7 reduce-scatter.11
where the time goes:
time: 2590 us; the launch traced here: 2580 us
  waiting for transfers between devices  2250 us (87%)
  matrix products  158 us (6%)
  other arithmetic  77.9 us (3%)
  blocking collectives  44.9 us (2%)
    reduce_scatter x1, waiting for transfers between devices, on_device(): lax.psum_scatter(grad_expand, ('dp', 'ctx'), scatter_dimension=0, tiled=T...  880 us
    reduce_scatter x1, waiting for transfers between devices, on_device(): lax.psum_scatter(grad_reduce, ('dp', 'ctx'), scatter_dimension=0, tiled=T...  438 us
    all_gather x1, waiting for transfers between devices, on_device(): lax.all_gather(expand_weight.astype(jnp.bfloat16), ('dp', 'ctx'), axis=0,...  233 us
    reduce_scatter x1, waiting for transfers between devices, on_device(): lax.psum_scatter(grad_input, ('dp', 'ctx'), scatter_dimension=0, tiled=True)  211 us
    reduce_scatter x1, waiting for transfers between devices, on_device(): lax.psum_scatter(pair_totals, 'ctx', scatter_dimension=1, tiled=True)  118 us
    all_gather x1, waiting for transfers between devices, on_device(): lax.all_gather(reduce_weight.astype(jnp.bfloat16), ('dp', 'ctx'), axis=0,...  117 us
    all_gather x1, waiting for transfers between devices, on_device(): lax.all_gather(input_weight.astype(jnp.bfloat16), ('dp', 'ctx'), axis=0,...  84.1 us
    reduce_scatter x1, waiting for transfers between devices, on_device(): lax.psum_scatter(grad_output, ('dp', 'ctx'), scatter_dimension=0, tiled=T...  74.5 us
  transfers between devices with their start and end apart: 10, of which 10 were waited for; matrix products, arithmetic and copies ran while one was open for 5% of the time, Pallas kernels for 0%

commit v1 on v0

v1 whole, which is shorter than its diff:
```python
import functools
import math

import jax
import jax.numpy as jnp
from jax import lax
from jax.experimental import pallas as pl
from jax.experimental.pallas import tpu as pltpu
from jax.sharding import Mesh
from jax.sharding import PartitionSpec as P

HEADS = 24
KV_HEADS = 6
HD = 64
FF = 5120
GROUP = 4
NPARAM = 39325824


EPSILON = 1e-06
THETA = 10000.0
MOMENTUM = 0.5

BF = jnp.bfloat16
F32 = jnp.float32
WIDE = 2 * HD
CHAIN = 4
CORES = 2
AXES = ("dp", "a", "b", "c")
ANY = pl.BlockSpec(memory_space=pl.ANY)
VMEM = pl.BlockSpec(memory_space=pltpu.VMEM)
NT = (((1,), (1,)), ((), ()))
TN = (((0,), (0,)), ((), ()))
NN = (((1,), (0,)), ((), ()))


def mm(left, right, dims):
    return lax.dot_general(left, right, dims, preferred_element_type=F32)


class Here:
    def __init__(self):
        self.y, self.a, self.b, self.c = (lax.axis_index(name) for name in AXES)
        self.dp, self.chain, self.mid, self.cores = (lax.axis_size(name) for name in AXES)
        self.rank = (self.a * self.mid + self.b) * self.cores + self.c
        self.shard = self.y * (self.chain * self.mid * self.cores) + self.rank

    def to(self, y=0, a=0, b=0, c=0):
        out = {}
        for name, mine, offset in zip(AXES, (self.y, self.a, self.b, self.c), (y, a, b, c)):
            out[name] = mine ^ offset if offset else mine
        return out

    def plane(self):
        return [
            (y, b) for y in range(self.dp) for b in range(self.mid) if y or b
        ]


def greet(here, offsets):
    barrier = pltpu.get_barrier_semaphore()
    for offset in offsets:
        pl.semaphore_signal(
            barrier, inc=1, device_id=here.to(**offset), device_id_type=pl.DeviceIdType.MESH
        )
    pl.semaphore_wait(barrier, len(offsets))


class Wire:
    def __init__(self, send, recv):
        self.send, self.recv, self.made = send, recv, []

    def push(self, source, target, device):
        k = len(self.made)
        copy = pltpu.make_async_remote_copy(
            src_ref=source,
            dst_ref=target,
            send_sem=self.send.at[k],
            recv_sem=self.recv.at[k],
            device_id=device,
            device_id_type=pl.DeviceIdType.MESH,
        )
        copy.start()
        self.made.append(copy)
        return copy

    def drain(self):
        for copy in self.made:
            copy.wait_send()


def wires(count):
    return [pltpu.SemaphoreType.DMA((count,)), pltpu.SemaphoreType.DMA((count,))]


def chain_offsets(here):
    return [dict(a=o) for o in range(1, here.chain)]


def plane_offsets(here):
    return [dict(y=y, b=b) for y, b in here.plane()]


def block_offsets(here):
    return [
        dict(y=y, b=b, c=c)
        for y in range(here.dp)
        for b in range(here.mid)
        for c in range(here.cores)
        if y or b or c
    ]


class Gather:
    def __init__(self, here, wire, shard, full):
        self.here, self.wire, self.shard, self.full = here, wire, shard, full
        self.core = []

    @staticmethod
    def copies(dp, chain, mid):
        return (chain - 1) + (dp * mid - 1) * chain + dp * chain * mid

    def spread(self, source, slot):
        h = self.here
        made = {
            (y, b): self.wire.push(source, slot, h.to(y=y, b=b)) for y, b in h.plane()
        }
        self.core.append(self.wire.push(source, slot, h.to(c=1)))
        return made

    def start(self):
        h = self.here
        slot = self.full.at[h.y, h.a, h.b, h.c]
        self.chain = {
            o: self.wire.push(self.shard, slot, h.to(a=o)) for o in range(1, h.chain)
        }
        self.sheet = {0: self.spread(self.shard, slot)}

    def relay_chain(self):
        h = self.here
        for o in range(1, h.chain):
            self.chain[o].wait_recv()
            slot = self.full.at[h.y, h.a ^ o, h.b, h.c]
            self.sheet[o] = self.spread(slot, slot)

    def relay_plane(self):
        h = self.here
        for o in range(h.chain):
            for y, b in h.plane():
                self.sheet[o][y, b].wait_recv()
                slot = self.full.at[h.y ^ y, h.a ^ o, h.b ^ b, h.c]
                self.core.append(self.wire.push(slot, slot, h.to(c=1)))

    def finish(self):
        for copy in self.core:
            copy.wait_recv()


def call(body, outs, ins, scratch, ident, out_specs, in_specs, sent=0):
    return pl.pallas_call(
        body,
        out_shape=outs,
        in_specs=in_specs,
        out_specs=out_specs,
        scratch_shapes=scratch,
        compiler_params=pltpu.CompilerParams(collective_id=ident, has_side_effects=True),
        cost_estimate=pl.CostEstimate(flops=0, bytes_accessed=sent, transcendentals=0),
    )(*ins)


def chunk_columns(chunk, part, width):
    start = part * FF + chunk * width
    return pl.ds(pl.multiple_of(start, 128), width)


def first_kernel(win_ref, ex_ref, win_out, e1_out, send, recv, local):
    h = Here()
    width = FF // (h.chain * h.cores)
    greet(h, [dict(a=a, c=c) for a in range(h.chain) for c in range(h.cores) if a or c] + plane_offsets(h))
    wire = Wire(send, recv)
    own = pltpu.make_async_copy(win_ref, win_out.at[h.y, h.a, h.b, h.c], local.at[0])
    own.start()
    gather = Gather(h, wire, win_ref, win_out)
    gather.start()
    kept = []
    for part in range(2):
        mine = ex_ref.at[:, chunk_columns(h.c * h.chain + h.a, part, width)]
        spot = e1_out.at[h.a, h.c, :, pl.ds(part * width, width)]
        copy = pltpu.make_async_copy(mine, spot, local.at[1 + part])
        copy.start()
        kept.append(copy)
    swaps = []
    for a in range(h.chain):
        for c in range(h.cores):
            if not (a or c):
                continue
            for part in range(2):
                chunk = (h.c ^ c) * h.chain + (h.a ^ a)
                source = ex_ref.at[:, chunk_columns(chunk, part, width)]
                spot = e1_out.at[h.a, h.c, :, pl.ds(part * width, width)]
                swaps.append(wire.push(source, spot, h.to(a=a, c=c)))
    gather.relay_chain()
    gather.relay_plane()
    gather.finish()
    for copy in swaps:
        copy.wait_recv()
    wire.drain()
    own.wait()
    for copy in kept:
        copy.wait()


def gather_first(win, ex, sizes):
    dp, chain, mid, cores = sizes
    rows = win.shape[0]
    width = 2 * FF // (chain * cores)
    count = Gather.copies(dp, chain, mid) + 2 * (chain * cores - 1)
    return call(
        first_kernel,
        (
            jax.ShapeDtypeStruct((dp, chain, mid, cores) + win.shape, BF),
            jax.ShapeDtypeStruct((chain, cores, rows, width), BF),
        ),
        (win, ex),
        wires(count) + [pltpu.SemaphoreType.DMA((3,))],
        1,
        (ANY, ANY),
        [ANY, ANY],
    )


def masked(values, pair, rank, span):
    key_pos = pair * (2 * span) + lax.broadcasted_iota(jnp.int32, values.shape, 0)
    query_pos = rank * span + lax.rem(lax.broadcasted_iota(jnp.int32, values.shape, 1), span)
    return jnp.where(key_pos <= query_pos, values, 0.0)


def second_kernel(
    q_ref, kv_ref, wout_ref, cot_ref, o_ref, lse_ref, kv_out, wout_out, cot_out,
    kv_all, send, recv, local,
):
    h = Here()
    span = kv_ref.shape[1]
    greet(
        h,
        chain_offsets(h) + plane_offsets(h) + [dict(c=1)],
    )
    wire = Wire(send, recv)
    own_out = pltpu.make_async_copy(wout_ref, wout_out.at[h.y, h.a, h.b, h.c], local.at[0])
    own_out.start()
    own_cot = pltpu.make_async_copy(cot_ref, cot_out.at[h.a, h.c], local.at[1])
    own_cot.start()

    def block(a, b, c):
        return kv_all.at[((h.a ^ a) * h.mid + (h.b ^ b)) * h.cores + (h.c ^ c)]

    mine = block(0, 0, 0)
    mine[...] = kv_ref[...]
    core = []
    chain = {o: wire.push(kv_ref, mine, h.to(a=o)) for o in range(1, h.chain)}
    side = {(0, b): wire.push(kv_ref, mine, h.to(b=b)) for b in range(1, h.mid)}
    core.append(wire.push(kv_ref, mine, h.to(c=1)))
    gather = Gather(h, wire, wout_ref, wout_out)
    for o in range(1, h.chain):
        chain[o].wait_recv()
        spot = block(o, 0, 0)
        for b in range(1, h.mid):
            side[o, b] = wire.push(spot, spot, h.to(b=b))
        core.append(wire.push(spot, spot, h.to(c=1)))
    gather.start()
    cots = {o: wire.push(cot_ref, cot_out.at[h.a, h.c], h.to(a=o)) for o in range(1, h.chain)}
    cot_core = [wire.push(cot_ref, cot_out.at[h.a, h.c], h.to(c=1))]
    for o in range(h.chain):
        for b in range(1, h.mid):
            side[o, b].wait_recv()
            spot = block(o, b, 0)
            core.append(wire.push(spot, spot, h.to(c=1)))
    gather.relay_chain()
    for copy in core:
        copy.wait_recv()
    store = pltpu.make_async_copy(kv_all, kv_out, local.at[2])
    store.start()

    last = h.rank // 2

    def head(g, unused):
        query = q_ref[g]

        def visit(pair, hide):
            keys = kv_all[pl.ds(2 * pair, 2), g].reshape(2 * span, WIDE)
            weights = jnp.exp(mm(keys, query, NT))
            if hide:
                weights = masked(weights, pair, h.rank, span)
            total = jnp.sum(weights, axis=0, keepdims=True)
            return total, mm(keys, weights.astype(BF), TN)[HD:]

        total, value = visit(last, True)
        lse_ref[g] = total
        o_ref[g] = value

        def step(pair, unused_inner):
            total, value = visit(pair, False)
            lse_ref[g] += total
            o_ref[g] += value
            return unused_inner

        lax.fori_loop(0, last, step, 0)
        o_ref[g] = o_ref[g] / lse_ref[g]
        lse_ref[g] = jnp.log(lse_ref[g])
        return unused

    lax.fori_loop(0, KV_HEADS, head, 0)
    gather.relay_plane()
    for o in range(1, h.chain):
        cots[o].wait_recv()
        spot = cot_out.at[h.a ^ o, h.c]
        cot_core.append(wire.push(spot, spot, h.to(c=1)))
    gather.finish()
    for copy in cot_core:
        copy.wait_recv()
    wire.drain()
    own_out.wait()
    own_cot.wait()
    store.wait()


def attend_forward(query, kv, wout, cot, sizes):
    dp, chain, mid, cores = sizes
    blocks = chain * mid * cores
    rows = query.shape[1]
    count = (
        (chain - 1) + (mid - 1) * chain + chain * mid
        + Gather.copies(dp, chain, mid) + 2 * (chain - 1) + 1
    )
    return call(
        second_kernel,
        (
            jax.ShapeDtypeStruct((KV_HEADS, HD, rows), F32),
            jax.ShapeDtypeStruct((KV_HEADS, 1, rows), F32),
            jax.ShapeDtypeStruct((blocks,) + kv.shape, BF),
            jax.ShapeDtypeStruct((dp, chain, mid, cores) + wout.shape, BF),
            jax.ShapeDtypeStruct((chain, cores) + cot.shape, BF),
        ),
        (query, kv, wout, cot),
        [pltpu.VMEM((blocks,) + kv.shape, BF)] + wires(count) + [pltpu.SemaphoreType.DMA((3,))],
        2,
        (VMEM, VMEM, ANY, ANY, ANY),
        [VMEM, VMEM, ANY, ANY],
    )


def third_kernel(n_ref, e1_ref, rd_ref, n_out, ex_out, rd_out, send, recv, rsend, rrecv, local):
    h = Here()
    greet(h, chain_offsets(h) + block_offsets(h))
    wire = Wire(send, recv)
    own = pltpu.make_async_copy(n_ref, n_out.at[h.a, h.c], local.at[0])
    own.start()
    rows = {o: wire.push(n_ref, n_out.at[h.a, h.c], h.to(a=o)) for o in range(1, h.chain)}
    core = [wire.push(n_ref, n_out.at[h.a, h.c], h.to(c=1))]
    kept, sheets = [], []
    for a in range(h.chain):
        for y, b in h.plane():
            sheets.append(wire.push(e1_ref.at[a], ex_out.at[h.y, a, h.b], h.to(y=y, b=b)))
        copy = pltpu.make_async_copy(e1_ref.at[a], ex_out.at[h.y, a, h.b], local.at[1 + a])
        copy.start()
        kept.append(copy)
    slot = h.b * h.cores + h.c

    def reduce_copy(number, y, b):
        device = h.to(y=y, b=b)
        device["c"] = h.y
        return pltpu.make_async_remote_copy(
            src_ref=rd_ref,
            dst_ref=rd_out.at[h.b, h.c],
            send_sem=rsend.at[number],
            recv_sem=rrecv.at[slot],
            device_id=device,
            device_id_type=pl.DeviceIdType.MESH,
        )

    far = [reduce_copy(1 + i, y, b) for i, (y, b) in enumerate(h.plane())]
    for copy in far:
        copy.start()

    @pl.when(h.c == h.y)
    def _():
        pltpu.make_async_copy(rd_ref, rd_out.at[h.b, h.c], rrecv.at[slot]).start()

    @pl.when(h.c != h.y)
    def _():
        reduce_copy(0, 0, 0).start()

    for o in range(1, h.chain):
        rows[o].wait_recv()
        spot = n_out.at[h.a ^ o, h.c]
        core.append(wire.push(spot, spot, h.to(c=1)))
    for copy in core:
        copy.wait_recv()
    for copy in sheets:
        copy.wait_recv()
    for b in range(h.mid):
        for c in range(h.cores):
            spot = rd_out.at[b, c]
            pltpu.make_async_copy(spot, spot, rrecv.at[b * h.cores + c]).wait()
    wire.drain()
    for copy in far:
        copy.wait_send()

    @pl.when(h.c != h.y)
    def _():
        reduce_copy(0, 0, 0).wait_send()

    own.wait()
    for copy in kept:
        copy.wait()


def gather_feed(normed, e1, rd, sizes):
    dp, chain, mid, cores = sizes
    count = 2 * (chain - 1) + 1 + chain * (dp * mid - 1)
    return call(
        third_kernel,
        (
            jax.ShapeDtypeStruct((chain, cores) + normed.shape, BF),
            jax.ShapeDtypeStruct((dp, chain, mid) + e1.shape[1:], BF),
            jax.ShapeDtypeStruct((mid, cores) + rd.shape, BF),
        ),
        (normed, e1, rd),
        wires(count)
        + [pltpu.SemaphoreType.DMA((dp * mid,)), pltpu.SemaphoreType.DMA((mid * cores,))]
        + [pltpu.SemaphoreType.DMA((1 + chain,))],
        3,
        (ANY, ANY, ANY),
        [ANY, ANY, ANY],
    )


class Fold:
    def __init__(self, here, wire, part, near, half, far):
        self.here, self.wire, self.part = here, wire, part
        self.near, self.half, self.far = near, half, far

    @staticmethod
    def copies(chain):
        return chain + chain - 1

    @staticmethod
    def scratch(part):
        chain, cores, rows, width = part.shape
        return [pltpu.VMEM((chain, rows, width), BF) for _ in range(3)]

    def start(self):
        h = self.here
        self.swap = {
            o: self.wire.push(self.part.at[h.a ^ o, h.c ^ 1], self.near.at[o], h.to(c=1))
            for o in list(range(1, h.chain)) + [0]
        }

    def pass_on(self):
        h = self.here
        self.sent = {}
        rows = self.part.shape[2]
        for o in range(1, h.chain):
            self.swap[o].wait_recv()

            def add(i, unused):
                at = pl.ds(pl.multiple_of(i * 16, 16), 16)
                both = self.part[h.a ^ o, h.c, at].astype(F32) + self.near[o, at].astype(F32)
                self.half[o, at] = both.astype(BF)
                return unused

            lax.fori_loop(0, rows // 16, add, 0)
            self.sent[o] = self.wire.push(self.half.at[o], self.far.at[o], h.to(a=o))
        self.swap[0].wait_recv()

    def finish(self, out):
        h = self.here
        rows = self.part.shape[2]
        for o in range(1, h.chain):
            self.sent[o].wait_recv()

        def add(i, unused):
            at = pl.ds(pl.multiple_of(i * 16, 16), 16)
            total = self.part[h.a, h.c, at].astype(F32) + self.near[0, at].astype(F32)
            for o in range(1, h.chain):
                total = total + self.far[o, at].astype(F32)
            out[at] = total
            return unused

        lax.fori_loop(0, rows // 16, add, 0)


def fold_offsets(here):
    return chain_offsets(here) + [dict(c=1)]


def fourth_kernel(part_ref, gr_ref, out_ref, gr_out, near, half, far, send, recv, gsend, grecv):
    h = Here()
    greet(h, chain_offsets(h) + block_offsets(h))
    wire = Wire(send, recv)
    fold = Fold(h, wire, part_ref, near, half, far)
    fold.start()
    slot = h.y * h.mid + h.b

    def chunk_copy(b, c):
        device = h.to(b=b, c=c)
        device["dp"] = h.c
        return pltpu.make_async_remote_copy(
            src_ref=gr_ref.at[h.b ^ b, h.c ^ c],
            dst_ref=gr_out.at[slot],
            send_sem=gsend.at[b * h.cores + c],
            recv_sem=grecv.at[slot],
            device_id=device,
            device_id_type=pl.DeviceIdType.MESH,
        )

    far_copies = [chunk_copy(b, c) for b in range(h.mid) for c in range(h.cores) if b or c]
    for copy in far_copies:
        copy.start()

    @pl.when(h.c == h.y)
    def _():
        pltpu.make_async_copy(gr_ref.at[h.b, h.c], gr_out.at[slot], grecv.at[slot]).start()

    @pl.when(h.c != h.y)
    def _():
        chunk_copy(0, 0).start()

    fold.pass_on()
    fold.finish(out_ref)
    for i in range(h.dp * h.mid):
        pltpu.make_async_copy(gr_out.at[i], gr_out.at[i], grecv.at[i]).wait()
    wire.drain()
    for copy in far_copies:
        copy.wait_send()

    @pl.when(h.c != h.y)
    def _():
        chunk_copy(0, 0).wait_send()


def fold_feed(part, gr, sizes):
    dp, chain, mid, cores = sizes
    return call(
        fourth_kernel,
        (
            jax.ShapeDtypeStruct(part.shape[2:], F32),
            jax.ShapeDtypeStruct((dp * mid,) + gr.shape[2:], BF),
        ),
        (part, gr),
        Fold.scratch(part)
        + wires(Fold.copies(chain))
        + [pltpu.SemaphoreType.DMA((mid * cores,)), pltpu.SemaphoreType.DMA((dp * mid,))],
        4,
        (VMEM, ANY),
        [VMEM, ANY],
    )


def fifth_kernel(
    q_ref, do_ref, lse_ref, delta_ref, kv_ref, part_ref, ge_ref,
    dq_ref, dkv_ref, out_ref, ge_out,
    made, got, near, half, far, send, recv, ksend, krecv,
):
    h = Here()
    span = kv_ref.shape[2]
    blocks = kv_ref.shape[0]
    greet(
        h,
        [
            dict(a=a, b=b, c=c)
            for a in range(h.chain)
            for b in range(h.mid)
            for c in range(h.cores)
            if a or b or c
        ]
        + [dict(y=y, b=b) for y, b in h.plane() if y],
    )
    wire = Wire(send, recv)
    fold = Fold(h, wire, part_ref, near, half, far)
    fold.start()
    sheets = []
    for i, (y, b) in enumerate(h.plane()):
        for a in range(h.chain):
            sheets.append(
                wire.push(ge_ref.at[h.y ^ y, a, h.b ^ b], ge_out.at[i, a], h.to(y=y, b=b))
            )
    fold.pass_on()

    last = h.rank // 2

    def visit(pair, hide):
        def head(g, unused):
            query, dout = q_ref[g], do_ref[g]
            keys = kv_ref[pl.ds(2 * pair, 2), g].reshape(2 * span, WIDE)
            probs = jnp.exp(mm(keys, query, NT) - lse_ref[g])
            if hide:
                probs = masked(probs, pair, h.rank, span)
            slope = probs * (mm(keys, dout, NT) - delta_ref[g])
            slope = slope.astype(BF)
            both = mm(slope, query, NN) + mm(probs.astype(BF), dout, NN)
            made[pl.ds(2 * pair, 2), g] = both.astype(BF).reshape(2, span, WIDE)
            add = mm(keys, slope, TN)[:HD]
            if hide:
                dq_ref[g] = add
            else:
                dq_ref[g] += add
            return unused

        lax.fori_loop(0, KV_HEADS, head, 0)

    def block_copy(o):
        peer = h.rank ^ o
        c, b, a = o % h.cores, (o // h.cores) % h.mid, o // (h.cores * h.mid)
        return pltpu.make_async_remote_copy(
            src_ref=made.at[peer],
            dst_ref=got.at[o],
            send_sem=ksend.at[o],
            recv_sem=krecv.at[o],
            device_id=h.to(a=a, b=b, c=c),
            device_id_type=pl.DeviceIdType.MESH,
        )

    visit(last, True)

    def step(pair, unused):
        visit(pair, False)
        return unused

    lax.fori_loop(0, last, step, 0)
    for o in range(1, blocks):

        @pl.when((h.rank ^ o) < h.rank)
        def _():
            block_copy(o).start()

    fold.finish(out_ref)
    dkv_ref[...] = made[h.rank].astype(F32)
    for o in range(1, blocks):

        @pl.when((h.rank ^ o) > h.rank)
        def _():
            block_copy(o).wait_recv()
            dkv_ref[...] += got[o].astype(F32)

        @pl.when((h.rank ^ o) < h.rank)
        def _():
            block_copy(o).wait_send()

    for copy in sheets:
        copy.wait_recv()
    wire.drain()


def attend_backward(query, dout, lse, delta, kv, part, ge, sizes):
    dp, chain, mid, cores = sizes
    blocks = chain * mid * cores
    rows = query.shape[1]
    others = dp * mid - 1
    return call(
        fifth_kernel,
        (
            jax.ShapeDtypeStruct((KV_HEADS, HD, rows), F32),
            jax.ShapeDtypeStruct(kv.shape[1:], F32),
            jax.ShapeDtypeStruct(part.shape[2:], F32),
            jax.ShapeDtypeStruct((others, chain) + ge.shape[3:], BF),
        ),
        (query, dout, lse, delta, kv, part, ge),
        [pltpu.VMEM(kv.shape, BF), pltpu.VMEM(kv.shape, BF)]
        + Fold.scratch(part)
        + wires(Fold.copies(chain) + others * chain)
        + wires(blocks),
        5,
        (VMEM, VMEM, VMEM, ANY),
        [VMEM, VMEM, VMEM, VMEM, VMEM, VMEM, ANY],
    )


class Scatter:
    def __init__(self, here, wire, grad, out, near, half, sheet, line, far, columns):
        self.here, self.wire, self.grad, self.out = here, wire, grad, out
        self.near, self.half, self.sheet, self.line, self.far = near, half, sheet, line, far
        self.columns = columns

    @staticmethod
    def copies(dp, chain, mid):
        return dp * mid + (dp * mid - 1) + (chain - 1)

    @staticmethod
    def scratch(grad):
        dp, chain, mid, cores, rows, width = grad.shape
        return [
            pltpu.VMEM((dp * mid, chain, rows, width), BF),
            pltpu.VMEM((dp * mid, chain, rows, width), BF),
            pltpu.VMEM((dp * mid, chain, rows, width), BF),
            pltpu.VMEM((chain, rows, width), BF),
            pltpu.VMEM((chain, rows, width), BF),
        ]

    def order(self):
        return self.here.plane() + [(0, 0)]

    def start(self):
        h = self.here
        self.swap = [
            self.wire.push(
                self.grad.at[h.y ^ y, :, h.b ^ b, h.c ^ 1, :, self.columns],
                self.near.at[i, :, :, self.columns],
                h.to(c=1),
            )
            for i, (y, b) in enumerate(self.order())
        ]

    def over_plane(self):
        h = self.here
        self.sent = []
        for i, (y, b) in enumerate(self.order()):
            self.swap[i].wait_recv()

            def add(a, unused):
                total = (
                    self.grad[h.y ^ y, a, h.b ^ b, h.c, :, self.columns].astype(F32)
                    + self.near[i, a, :, self.columns].astype(F32)
                )
                self.half[i, a, :, self.columns] = total.astype(BF)
                return unused

            lax.fori_loop(0, h.chain, add, 0)
            if y or b:
                self.sent.append(
                    self.wire.push(
                        self.half.at[i, :, :, self.columns],
                        self.sheet.at[i, :, :, self.columns],
                        h.to(y=y, b=b),
                    )
                )

    def over_chain(self):
        h = self.here
        own = len(self.order()) - 1
        for copy in self.sent:
            copy.wait_recv()
        self.last = []
        for o in list(range(1, h.chain)) + [0]:
            total = self.half[own, h.a ^ o, :, self.columns].astype(F32)
            for i in range(own):
                total = total + self.sheet[i, h.a ^ o, :, self.columns].astype(F32)
            if o:
                self.line[o, :, self.columns] = total.astype(BF)
                self.last.append(
                    self.wire.push(
                        self.line.at[o, :, self.columns],
                        self.far.at[o, :, self.columns],
                        h.to(a=o),
                    )
                )
            else:
                self.out[:, self.columns] = total

    def finish(self):
        h = self.here
        for copy in self.last:
            copy.wait_recv()
        total = self.out[:, self.columns]
        for o in range(1, h.chain):
            total = total + self.far[o, :, self.columns].astype(F32)
        self.out[:, self.columns] = total


def sixth_kernel(
    gi_ref, go_ref, ge_ref, gi_out, go_out, ge_out,
    n1, h1, s1, l1, f1, n2, h2, s2, l2, f2, send, recv, local,
):
    h = Here()
    greet(
        h,
        [dict(a=a, c=c) for a in range(h.chain) for c in range(h.cores) if a or c]
        + plane_offsets(h),
    )
    wire = Wire(send, recv)
    width = FF // (h.chain * h.cores)
    jobs = [
        Scatter(h, wire, gi_ref, gi_out, n1, h1, s1, l1, f1, columns)
        for columns in (pl.ds(0, gi_ref.shape[-1] // 2), pl.ds(gi_ref.shape[-1] // 2, gi_ref.shape[-1] // 2))
    ] + [Scatter(h, wire, go_ref, go_out, n2, h2, s2, l2, f2, pl.ds(0, go_ref.shape[-1]))]
    for job in jobs:
        job.start()
    kept, swaps = [], []
    chunk = h.c * h.chain + h.a
    for a in range(h.chain):
        for c in range(h.cores):
            for part in range(2):
                source = ge_ref.at[h.a ^ a, h.c ^ c, :, pl.ds(part * width, width)]
                spot = ge_out.at[:, chunk_columns(chunk, part, width)]
                if a or c:
                    swaps.append(wire.push(source, spot, h.to(a=a, c=c)))
                else:
                    copy = pltpu.make_async_copy(source, spot, local.at[part])
                    copy.start()
                    kept.append(copy)
    jobs[0].over_plane()
    jobs[1].over_plane()
    jobs[2].over_plane()
    for job in jobs:
        job.over_chain()
    for job in jobs:
        job.finish()
    for copy in swaps:
        copy.wait_recv()
    wire.drain()
    for copy in kept:
        copy.wait()


def scatter_projections(gi, go, ge, sizes):
    dp, chain, mid, cores = sizes
    count = 3 * Scatter.copies(dp, chain, mid) + 2 * (chain * cores - 1)
    return call(
        sixth_kernel,
        (
            jax.ShapeDtypeStruct(gi.shape[4:], F32),
            jax.ShapeDtypeStruct(go.shape[4:], F32),
            jax.ShapeDtypeStruct((ge.shape[2], 2 * FF), BF),
        ),
        (gi, go, ge),
        Scatter.scratch(gi)
        + Scatter.scratch(go)
        + wires(count)
        + [pltpu.SemaphoreType.DMA((2,))],
        6,
        (VMEM, VMEM, ANY),
        [VMEM, VMEM, ANY],
    )


def seventh_kernel(x_ref, out_ref, got, send, recv):
    h = Here()
    offsets = [
        dict(y=y, a=a, b=b, c=c)
        for y in range(h.dp)
        for a in range(h.chain)
        for b in range(h.mid)
        for c in range(h.cores)
        if y or a or b or c
    ]
    greet(h, offsets)
    wire = Wire(send, recv)
    copies = [wire.push(x_ref, got.at[h.shard], h.to(**offset)) for offset in offsets]
    got[h.shard] = x_ref[...]
    for copy in copies:
        copy.wait_recv()
    out_ref[...] = jnp.sum(got[...], axis=0)
    wire.drain()


def total_of(x, sizes):
    count = math.prod(sizes)
    return call(
        seventh_kernel,
        jax.ShapeDtypeStruct(x.shape, F32),
        (x,),
        [pltpu.VMEM((count,) + x.shape, F32)] + wires(count),
        7,
        VMEM,
        [VMEM],
    )


def rms_normed(values, gains):
    mean_square = jnp.mean(values * values, axis=-1, keepdims=True)
    return values * lax.rsqrt(mean_square + EPSILON) * gains


def rotary(values, positions):
    half_width = values.shape[-1] // 2
    frequency = THETA ** (-2.0 * jnp.arange(half_width).astype(F32) / values.shape[-1])
    angles = positions.astype(F32)[:, None] * frequency[None, :]
    cosine = jnp.cos(angles)[:, None, :]
    sine_rows = jnp.sin(angles)[:, None, :]
    front_half = values[..., :half_width]
    back_half = values[..., half_width:]
    return jnp.concatenate(
        [front_half * cosine - back_half * sine_rows, back_half * cosine + front_half * sine_rows],
        axis=-1,
    )


def prepare(projected, head_gains, positions):
    row_count = projected.shape[0]
    queries = projected[:, : HEADS * HD].reshape(row_count, HEADS, HD)
    key_rows = projected[:, HEADS * HD : (HEADS + KV_HEADS) * HD].reshape(row_count, KV_HEADS, HD)
    value_rows = projected[:, (HEADS + KV_HEADS) * HD :].reshape(row_count, KV_HEADS, HD)
    queries = rotary(rms_normed(queries, head_gains[0]), positions)
    key_rows = rotary(rms_normed(key_rows, head_gains[1]), positions)
    return (queries, key_rows, value_rows)


def by_group(values):
    rows = values.shape[0]
    values = values.reshape(rows, KV_HEADS, GROUP, HD).transpose(1, 2, 0, 3)
    return values.reshape(KV_HEADS, GROUP * rows, HD)


def by_row(values, rows):
    values = values.reshape(KV_HEADS, HD, GROUP, rows).transpose(3, 0, 2, 1)
    return values.reshape(rows, HEADS * HD)


def on_device(
    sizes,
    tokens,
    cotangent,
    norm_gains,
    head_gains,
    input_weight,
    output_weight,
    expand_weight,
    reduce_weight,
    norm_moment,
    head_moment,
    input_moment,
    output_moment,
    expand_moment,
    reduce_moment,
    learn_rate,
):
    dp, chain, mid, cores = sizes
    seq_count, rows, model_width = tokens.shape
    assert seq_count == 1
    place = (lax.axis_index("a") * mid + lax.axis_index("b")) * cores + lax.axis_index("c")
    positions = place * rows + jnp.arange(rows, dtype=jnp.int32)
    score_scale = 1.0 / math.sqrt(HD)
    upstream_low = cotangent.reshape(rows, model_width)

    full_input, e1 = gather_first(input_weight.astype(BF), expand_weight.astype(BF), sizes)
    full_input = full_input.reshape(model_width, -1)
    input_rows = tokens.reshape(rows, model_width).astype(F32)
    normed_one, norm_one_pull = jax.vjp(rms_normed, input_rows, norm_gains[0])
    normed_one = normed_one.astype(BF)
    projected = jnp.dot(normed_one, full_input, preferred_element_type=F32)

    def prepare_here(projected_rows, gains):
        return prepare(projected_rows, gains, positions)

    (queries, key_rows, value_rows), prepare_pull = jax.vjp(prepare_here, projected, head_gains)
    query_low = by_group((queries.astype(BF) * score_scale).reshape(rows, HEADS * HD))
    query_wide = jnp.pad(query_low, ((0, 0), (0, 0), (0, HD)))
    kv_low = jnp.concatenate([key_rows, value_rows], axis=-1).astype(BF).transpose(1, 0, 2)

    attended_cols, log_mass, kv_all, full_output, cot_all = attend_forward(
        query_wide, kv_low, output_weight.astype(BF), upstream_low, sizes
    )
    full_output = full_output.reshape(-1, model_width)
    attended = by_row(attended_cols, rows)
    attended_low = attended.astype(BF)
    branch = jnp.dot(attended_low, full_output, preferred_element_type=F32)
    residual = input_rows + branch
    normed_two, norm_two_pull = jax.vjp(rms_normed, residual, norm_gains[1])
    normed_two = normed_two.astype(BF)

    n_all, ex_all, rd_all = gather_feed(normed_two, e1, reduce_weight.astype(BF), sizes)
    n_all = n_all.reshape(-1, model_width)
    cot_all = cot_all.reshape(-1, model_width)
    ex_all = ex_all.reshape(model_width, -1)
    rd_all = rd_all.reshape(-1, model_width)
    part_width = rd_all.shape[0]
    expanded = jnp.dot(n_all, ex_all, preferred_element_type=F32)
    gate_value = expanded[:, :part_width]
    up_value = expanded[:, part_width:]
    sigmoid = jax.nn.sigmoid(gate_value)
    activated = gate_value * sigmoid
    slope = sigmoid * (1.0 + gate_value * (1.0 - sigmoid))
    hidden = (activated * up_value).astype(BF)
    hidden_grad = jnp.einsum("rd,fd->rf", cot_all, rd_all, preferred_element_type=F32)
    expand_grad = jnp.concatenate(
        [hidden_grad * up_value * slope, hidden_grad * activated], axis=1
    ).astype(BF)
    back_part = jnp.einsum("rf,df->rd", expand_grad, ex_all, preferred_element_type=F32).astype(BF)
    grad_reduce = jnp.einsum("rf,rd->fd", hidden, cot_all, preferred_element_type=F32).astype(BF)
    normed_two_grad, reduce_got = fold_feed(
        back_part.reshape(chain, cores, rows, model_width),
        grad_reduce.reshape(mid, cores, -1, model_width),
        sizes,
    )
    out_part = jnp.dot(hidden, rd_all, preferred_element_type=F32).astype(BF)
    grad_expand = jnp.einsum("rd,rf->df", n_all, expand_grad, preferred_element_type=F32).astype(BF)

    residual_part, gain_two_grad = norm_two_pull(normed_two_grad)
    residual_grad = upstream_low.astype(F32) + residual_part
    branch_grad = residual_grad.astype(BF)
    grad_output = jnp.einsum("rh,rd->hd", attended_low, branch_grad, preferred_element_type=F32)
    attended_grad = jnp.einsum(
        "rd,hd->rh", branch_grad, full_output, preferred_element_type=F32
    ).astype(BF)
    row_delta = jnp.sum(
        (attended_grad.astype(F32) * attended).reshape(rows, KV_HEADS, GROUP, HD), axis=-1
    )
    row_delta = row_delta.transpose(1, 2, 0).reshape(KV_HEADS, 1, GROUP * rows)
    dout_wide = jnp.pad(by_group(attended_grad), ((0, 0), (0, 0), (HD, 0)))
    grad_expand = grad_expand.reshape(dp, chain, mid, cores, -1, grad_expand.shape[1])
    query_cols, kv_grad, result, expand_got = attend_backward(
        query_wide,
        dout_wide,
        log_mass,
        row_delta,
        kv_all,
        out_part.reshape(chain, cores, rows, model_width),
        grad_expand,
        sizes,
    )
    query_grads = by_row(query_cols, rows) * score_scale
    kv_grad = kv_grad.transpose(1, 0, 2)
    projected_grad, head_grads = prepare_pull(
        (query_grads.reshape(rows, HEADS, HD), kv_grad[..., :HD], kv_grad[..., HD:])
    )
    projected_low = projected_grad.astype(BF)
    grad_input = jnp.einsum("rd,rc->dc", normed_one, projected_low, preferred_element_type=F32)
    normed_one_grad = jnp.einsum(
        "rc,dc->rd", projected_low, full_input, preferred_element_type=F32
    )
    input_part, gain_one_grad = norm_one_pull(normed_one_grad)
    token_low = (residual_grad + input_part).astype(BF).reshape(tokens.shape)
    layer_out = (residual + result).astype(BF).reshape(tokens.shape)

    y_here, b_here = lax.axis_index("dp"), lax.axis_index("b")
    own_expand = lax.dynamic_index_in_dim(grad_expand, y_here, 0, keepdims=False)
    own_expand = lax.dynamic_index_in_dim(own_expand, b_here, 1, keepdims=False)
    sum_expand = own_expand.astype(F32) + jnp.sum(expand_got.astype(F32), axis=0)
    shard_reduce = jnp.sum(reduce_got.astype(F32), axis=0)

    def sharded(grad):
        return grad.astype(BF).reshape(dp, chain, mid, cores, -1, grad.shape[1])

    shard_input, shard_output, shard_expand = scatter_projections(
        sharded(grad_input), sharded(grad_output), sum_expand.astype(BF), sizes
    )
    shard_expand = shard_expand.astype(F32)
    squares_local = (
        jnp.sum(shard_input * shard_input)
        + jnp.sum(shard_output * shard_output)
        + jnp.sum(shard_expand * shard_expand)
        + jnp.sum(shard_reduce * shard_reduce)
    )
    gain_count = norm_gains.size
    head_count = head_gains.size
    packed = jnp.concatenate(
        [
            gain_one_grad,
            gain_two_grad,
            head_grads.reshape(-1),
            jnp.full((128,), squares_local, F32),
        ]
    ).reshape(-1, 128)
    packed = jnp.pad(packed, ((0, -packed.shape[0] % 8), (0, 0)))
    totals = total_of(packed, sizes).reshape(-1)
    gain_totals = totals[:gain_count].reshape(norm_gains.shape)
    head_totals = totals[gain_count : gain_count + head_count].reshape(head_gains.shape)
    square_total = totals[gain_count + head_count]
    grad_norm = jnp.sqrt(
        square_total + jnp.sum(gain_totals * gain_totals) + jnp.sum(head_totals * head_totals)
    )
    clip_limit = math.sqrt(NPARAM)
    factor = clip_limit / jnp.maximum(grad_norm, clip_limit)

    def advance(weight, moment, gradient):
        new_moment = MOMENTUM * moment + factor * gradient
        return (new_moment, weight - learn_rate * new_moment)

    moment_norms, next_norms = advance(norm_gains, norm_moment, gain_totals)
    moment_heads, next_heads = advance(head_gains, head_moment, head_totals)
    moment_input, next_input = advance(input_weight, input_moment, shard_input)
    moment_output, next_output = advance(output_weight, output_moment, shard_output)
    moment_expand, next_expand = advance(expand_weight, expand_moment, shard_expand)
    moment_reduce, next_reduce = advance(reduce_weight, reduce_moment, shard_reduce)
    return (
        layer_out,
        token_low,
        grad_norm,
        moment_norms,
        moment_heads,
        moment_input,
        moment_output,
        moment_expand,
        moment_reduce,
        next_norms,
        next_heads,
        next_input,
        next_output,
        next_expand,
        next_reduce,
    )


def solution(mesh):
    dp, ctx = mesh.shape["dp"], mesh.shape["ctx"]
    sizes = (dp, CHAIN, ctx // (CHAIN * CORES), CORES)
    assert dp == CORES
    grid = Mesh(mesh.devices.reshape(sizes), AXES)
    rows = P("dp", ("a", "b", "c"), None)
    shard = P(AXES, None)
    in_specs = (rows, rows, P(), P(), shard, shard, shard, shard)
    in_specs += (P(), P(), shard, shard, shard, shard, P())
    out_specs = (rows, rows, P(), P(), P(), shard, shard, shard, shard)
    out_specs += (P(), P(), shard, shard, shard, shard)
    return jax.shard_map(
        functools.partial(on_device, sizes),
        mesh=grid,
        in_specs=in_specs,
        out_specs=out_specs,
        check_vma=False,
    )
```

time: 2590 us -> 728 us (0.28)
  waiting for transfers between devices: 2250 us -> 0 us
  Pallas kernels: 0 us -> 558 us
  matrix products: 158 us -> 71.5 us
  blocking collectives: 44.9 us -> 0 us
    reduce_scatter x5 -> x0, waiting for transfers between devices: 1720 us -> none  [the longest x1 880 us: on_device(): lax.psum_scatter(grad_expand, ('dp', 'ctx'), scatter_dimension=0, tiled=T...]
    pallas_call x0 -> x7, Pallas kernels: none -> 558 us  [call(): pl.pallas_call(body, out_shape=outs, in_specs=in_specs, out_specs=out_spe...]
    all_gather x5 -> x0, waiting for transfers between devices: 531 us -> none  [the longest x1 233 us: on_device(): lax.all_gather(expand_weight.astype(jnp.bfloat16), ('dp', 'ctx'), axis=0,...]
    dot_general x17 -> x8, matrix products: 133 us -> 46.4 us  [the longest x1 9.15 us: on_device(): expanded = jnp.dot(n_all, ex_all, preferred_element_type=F32)]
    psum x1 -> x0, blocking collectives: 44.9 us -> none  [on_device(): lax.psum((jnp.stack([gain_one_grad, gain_two_grad]), head_grads, squares_...]
    dynamic_update_slice x16 -> x0, other arithmetic: 29.4 us -> none  [back_one_block(): lax.dynamic_update_slice_in_dim(pair_totals, stored + pair_add, block_tur...]
  transfers between devices with their start and end apart: 10 -> 0, of which waited for: 10 -> 0; matrix products, arithmetic and copies ran while one was open for 5% -> 0% of each run, Pallas kernels for 0% -> 0%
where the time goes in v1:
time: 728 us; the launch traced here: 722 us
  Pallas kernels  558 us (77%)
  matrix products  71.5 us (10%)
  other arithmetic  56.5 us (8%)
  local copies, waits for them, and re-layouts  27.9 us (4%)
  between operations  8.24 us (1%)
    pallas_call x7, Pallas kernels, call(): pl.pallas_call(body, out_shape=outs, in_specs=in_specs, out_specs=out_spe...  558 us

profile of v1, /device:TPU:0, one launch (start us, length us, event | category | flops | bytes accessed | tf_op | source)
XLA Modules:
  0.0 721.9 jit_solution(4654997615822728140)
XLA Ops:
  2.7 3.0 convert_element_type.132.ex_ref
  6.5 63.4 %shard_map.262 = (bf16[2,4,2,2,64,2304]{5,4,3,2,1,0:T(8,128)(2,1)}, bf16[4,2,64,1280]{3,2,1,0:T(8,128)(2,1)}) custom-call(bf16[64,2304]{1,0:T(8,128)(2,1)} %convert_element_type.131.win_ref, bf16[64,10240]{1,0:T(8,128)(2,1)} %convert_element_type.132.ex_ref), custom_call_target="tpu_custom_call" | custom-call | tf_op jit(solution)/shard_map/pallas_call | solution.py:160
  69.9 5.1 fusion.22
  86.3 79.5 %shard_map.263 = (f32[6,64,512]{2,1,0:T(8,128)}, f32[6,1,512]{2,1,0:T(1,128)}, bf16[16,6,128,128]{3,2,1,0:T(8,128)(2,1)}, bf16[2,4,2,2,48,2048]{5,4,3,2,1,0:T(8,128)(2,1)}, bf16[4,2,128,2048]{3,2,1,0:T(8,128)(2,1)}) custom-call(bf16[6,512,128]{2,1,0:T(8,128)(2,1)} %pad.39.q_ref, bf16[6,128,128]{2,1,0:T(8,128)(2,1)} %maximum_bitcast_fusion.kv_ref, ...), custom_call_target="tpu_custom_call" | custom-call | tf_op jit(solution)/shard_map/pallas_call | solution.py:160
  167.0 4.0 multiply_reduce_fusion.3
  172.9 96.9 %shard_map.264 = (bf16[4,2,128,2048]{3,2,1,0:T(8,128)(2,1)}, bf16[2,4,2,2,64,1280]{5,4,3,2,1,0:T(8,128)(2,1)}, bf16[2,2,160,2048]{3,2,1,0:T(8,128)(2,1)}) custom-call(bf16[128,2048]{1,0:T(8,128)(2,1)} %multiply_convert_fusion.3.n_ref, bf16[4,2,64,1280]{3,2,1,0:T(8,128)(2,1)} %get-tuple-element.38.e1_ref, bf16[160,2048]{1,0:T(8,128)(2,1)} %convert_element_type.140.rd_ref), custom_call_target="tpu_custom_call" | custom-call | tf_op jit(solution)/shard_map/pallas_call | solution.py:160
  269.8 9.2 %fusion.41 = f32[1024,1280]{0,1:T(8,128)S(1)} fusion(bf16[1024,2048]{1,0:T(8,128)(2,1)} %bitcast.184, bf16[2048,1280]{1,0:T(8,128)(2,1)} %bitcast.178), kind=kOutput, calls=%fused_computation.128 | convolution fusion | flops 5368709120 | bytes 14680064 | tf_op jit(solution)/shard_map/dot_general | solution.py:967
  279.0 3.8 multiply_convert_fusion.2
  282.8 7.4 %convolution_convert_fusion.2 = bf16[2048,1280]{1,0:T(8,128)(2,1)} fusion(bf16[1024,2048]{1,0:T(8,128)(2,1)S(1)} %bitcast.185, bf16[1024,640]{0,1:T(8,128)(2,1)S(1)} %get-tuple-element.74, bf16[1024,640]{0,1:T(8,128)(2,1)S(1)} %get-tuple-element.73), kind=kOutput, calls=%fused_computation.3 | convolution fusion | flops 5376573440 | bytes 12058624 | tf_op jit(solution)/shard_map/rd,rf->df/dot_general | solution.py:986
  290.3 5.4 convolution_convert_fusion.3
  295.7 4.1 convolution_convert_fusion.5
  299.9 7.3 %convolution_convert_fusion.4 = bf16[1024,2048]{1,0:T(8,128)(2,1)} fusion(bf16[2048,1280]{1,0:T(8,128)(2,1)S(1)} %bitcast.181, bf16[1024,640]{0,1:T(8,128)(2,1)S(1)} %get-tuple-element.74, bf16[1024,640]{0,1:T(8,128)(2,1)S(1)} %get-tuple-element.73), kind=kOutput, calls=%fused_computation.6 | convolution fusion | flops 5376049152 | bytes 12058624 | tf_op jit(solution)/shard_map/rf,df->rd/dot_general | solution.py:978
  307.1 45.9 %shard_map.265 = (f32[128,2048]{1,0:T(8,128)}, bf16[4,160,2048]{2,1,0:T(8,128)(2,1)}) custom-call(bf16[4,2,128,2048]{3,2,1,0:T(8,128)(2,1)} %bitcast.146, bf16[2,2,160,2048]{3,2,1,0:T(8,128)(2,1)} %bitcast.155), custom_call_target="tpu_custom_call" | custom-call | tf_op jit(solution)/shard_map/pallas_call | solution.py:160
  353.0 2.2 multiply_reduce_fusion.1
  357.6 2.3 copy.73
  359.9 6.2 convert_multiply_fusion.3
  370.1 2.3 pad.40.do_ref
  372.4 2.3 copy.74
  376.5 119.4 %shard_map.266 = (f32[6,64,512]{2,1,0:T(8,128)}, f32[6,128,128]{2,1,0:T(8,128)}, f32[128,2048]{1,0:T(8,128)}, bf16[3,4,2,64,1280]{4,3,2,1,0:T(8,128)(2,1)}) custom-call(bf16[6,512,128]{2,1,0:T(8,128)(2,1)} %pad.39.q_ref, bf16[6,512,128]{2,1,0:T(8,128)(2,1)} %pad.40.do_ref, f32[6,1,512]{2,1,0:T(1,128)} %get-tuple-element.43.lse_ref, f32[6,1,512]{2,1,0:T(1,128)} %bitcast.175, ...), custom_call_target="tpu_custom_call" | custom-call | tf_op jit(solution)/shard_map/pallas_call | solution.py:160
  500.4 4.5 convert_reduce_fusion
  504.9 3.5 fusion.2.ge_ref
  508.5 4.4 convolution_convert_fusion.1
  516.0 2.3 add_add_fusion.2
  518.6 6.4 convolution_convert_fusion
  525.0 130.2 %shard_map.267 = (f32[64,2304]{1,0:T(8,128)}, f32[48,2048]{1,0:T(8,128)}, bf16[64,10240]{1,0:T(8,128)(2,1)}) custom-call(bf16[2,4,2,2,64,2304]{5,4,3,2,1,0:T(8,128)(2,1)} %bitcast.132, bf16[2,4,2,2,48,2048]{5,4,3,2,1,0:T(8,128)(2,1)} %bitcast.135, bf16[4,2,64,1280]{3,2,1,0:T(8,128)(2,1)} %fusion.2.ge_ref), custom_call_target="tpu_custom_call" | custom-call | tf_op jit(solution)/shard_map/pallas_call | solution.py:160
  660.0 2.6 fusion
  663.3 2.4 convert_reduce_fusion.1
  668.4 8.1 %fusion.10 = (f32[2048]{0:T(1024)S(1)}, f32[128]{0:T(128)S(1)}, f32[128,2048]{1,0:T(8,128)}) fusion(bf16[1,128,2048]{2,1,0:T(8,128)(2,1)S(1)} %copy-done, f32[128]{0:T(128)S(1)} %copy-done.48, f32[2048]{0:T(1024)S(1)} %bitcast.168, bf16[2048,2304]{1,0:T(8,128)(2,1)} %bitcast.131, f32[128,1536]{0,1:T(8,128)S(1)} %bitcast.145, f32[128,384]{0,1:T(8,128)} %bitcast.158, ...), kind=kOutput, calls=%fused_computation.38 | convolution fusion | flops 1210677120 | bytes 12207104 | tf_op jit(solution)/shard_map/rc,dc->rd/dot_general | solution.py:1018
  677.2 22.5 %shard_map.268 = f32[40,128]{1,0:T(8,128)} custom-call(f32[40,128]{1,0:T(8,128)} %pad.50.x_ref), custom_call_target="tpu_custom_call" | custom-call | tf_op jit(solution)/shard_map/pallas_call | solution.py:160
  706.2 4.3 multiply_subtract_fusion.1
  711.1 3.0 multiply_subtract_fusion
  717.7 2.9 fusion.19
  (206 shorter events, 46.8 us)
Async XLA Ops:
  0.6 5.1 copy-start.19
  2.7 67.2 %copy-start.59 = (f32[128]{0:T(128)}, f32[128]{0:T(128)S(1)}, u32[]{:S(2)}) copy-start(f32[128]{0:T(128)S(1)} %fusion.12) | copy-start | bytes 1540
  2.7 67.2 %copy-start.47 = (f32[128]{0:T(128)}, f32[128]{0:T(128)S(1)}, u32[]{:S(2)}) copy-start(f32[128]{0:T(128)S(1)} %fusion.34) | copy-start | bytes 1540
  2.7 67.2 %copy-start = (bf16[1,128,2048]{2,1,0:T(8,128)(2,1)S(1)}, bf16[1,128,2048]{2,1,0:T(8,128)(2,1)}, u32[]{:S(2)}) copy-start(bf16[1,128,2048]{2,1,0:T(8,128)(2,1)} %param.15) | copy-start | bytes 1572868
  69.9 5.5 copy-start.56
  75.5 4.3 copy-start.5
  167.0 5.0 copy-start.8
  171.0 182.0 %copy-start.55 = (f32[128]{0:T(128)}, f32[128]{0:T(128)S(1)}, u32[]{:S(2)}) copy-start(f32[128]{0:T(128)S(1)} %fusion.35) | copy-start | bytes 1540
  269.8 9.2 %copy-start.61 = (bf16[4,2,128,2048]{3,2,1,0:T(8,128)(2,1)S(1)}, bf16[4,2,128,2048]{3,2,1,0:T(8,128)(2,1)}, u32[]{:S(2)}) copy-start(bf16[4,2,128,2048]{3,2,1,0:T(8,128)(2,1)} %get-tuple-element.37) | copy-start | bytes 12582916
  269.8 9.2 %copy-start.63 = (bf16[2,2,160,2048]{3,2,1,0:T(8,128)(2,1)S(1)}, bf16[2,2,160,2048]{3,2,1,0:T(8,128)(2,1)}, u32[]{:S(2)}) copy-start(bf16[2,2,160,2048]{3,2,1,0:T(8,128)(2,1)} %get-tuple-element.39) | copy-start | bytes 7864324
  290.3 9.6 %slice-start = ((s8[5242880]{0:T(1024)(128)(4,1)}), s8[4194304]{0:T(1024)(128)(4,1)S(1)}, s32[]{:S(2)}) async-start(s8[5242880]{0:T(1024)(128)(4,1)} %bitcast.179), calls=%async_computation | async-start | bytes 8388608
  295.7 4.1 slice-start.1
  376.5 120.8 %copy-start.42 = (f32[128,6]{0,1:T(8,128)S(1)}, f32[128,6]{0,1:T(8,128)}, u32[]{:S(2)}) copy-start(f32[128,6]{0,1:T(8,128)} %copy-done.41) | copy-start | bytes 9220
  376.5 120.8 %copy-start.51 = (f32[64]{0:T(128)S(1)}, f32[64]{0:T(128)}, u32[]{:S(2)}) copy-start(f32[64]{0:T(128)} %copy-done.50) | copy-start | bytes 772
  495.9 4.1 copy-start.36
  495.9 4.1 copy-start.53
  508.4 4.5 copy-start.45
  508.4 4.5 copy-start.6
  508.4 4.5 copy-start.14
  508.4 4.5 copy-start.16
  508.5 7.5 %copy-start.40 = (f32[128,24]{0,1:T(8,128)S(1)}, f32[128,24]{0,1:T(8,128)}, u32[]{:S(2)}) copy-start(f32[128,24]{0,1:T(8,128)} %copy-done.39) | copy-start | bytes 36868
  508.5 7.5 %copy-start.37 = (f32[128,24]{0,1:T(8,128)S(1)}, f32[128,24]{0,1:T(8,128)}, u32[]{:S(2)}) copy-start(f32[128,24]{0,1:T(8,128)} %copy-done.35) | copy-start | bytes 36868
  508.5 7.5 %copy-start.54 = (f32[64]{0:T(128)S(1)}, f32[64]{0:T(128)}, u32[]{:S(2)}) copy-start(f32[64]{0:T(128)} %get-tuple-element.87) | copy-start | bytes 772
  513.0 5.6 copy-start.48
  518.6 6.4 copy-start.22
  663.3 5.1 copy-start.4
  668.4 8.1 %copy-start.46 = (f32[2048]{0:T(1024)S(1)}, f32[2048]{0:T(1024)}, u32[]{:S(2)}) copy-start(f32[2048]{0:T(1024)} %get-tuple-element.53) | copy-start | bytes 24580
  706.2 4.3 copy-start.3
  706.2 4.3 copy-start.7
  706.2 4.9 copy-start.18
  711.1 4.1 copy-start.20
  711.1 4.1 copy-start.21
  (34 other events, 79.0 us)

commit v2 on v1

--- a/solution.py
+++ b/solution.py
@@ -111,60 +111,191 @@
     ]
 
 
+def planar(here, number):
+    pair = [("b", here.mid), ("y", here.dp)]
+    return pair if number % 2 == 0 else pair[::-1]
+
+
+class Sheet:
+    def __init__(self, here, wire, spot):
+        self.here, self.wire, self.spot = here, wire, spot
+        self.first, self.second = {}, {}
+
+    def start(self, number, source):
+        h = self.here
+        (one, n_one), (two, n_two) = planar(h, number)
+        slot = self.spot(number, 0, 0)
+        for k in range(1, n_one):
+            self.first[number, k] = self.wire.push(source, slot, h.to(**{one: k}))
+        for s in range(1, n_two):
+            self.second[number, 0, s] = self.wire.push(source, slot, h.to(**{two: s}))
+
+    def relay(self, number, landed=None):
+        h = self.here
+        (one, n_one), (two, n_two) = planar(h, number)
+        for k in range(1, n_one):
+            self.first[number, k].wait_recv()
+            slot = self.spot(number, *self.place(one, k))
+            for s in range(1, n_two):
+                self.second[number, k, s] = self.wire.push(slot, slot, h.to(**{two: s}))
+            if landed:
+                landed(slot)
+
+    def finish(self, number, landed=None):
+        h = self.here
+        (one, n_one), (two, n_two) = planar(h, number)
+        for k in range(n_one):
+            for s in range(1, n_two):
+                self.second[number, k, s].wait_recv()
+                if landed:
+                    y1, b1 = self.place(one, k)
+                    y2, b2 = self.place(two, s)
+                    landed(self.spot(number, y1 + y2, b1 + b2))
+
+    @staticmethod
+    def place(name, offset):
+        return (offset, 0) if name == "y" else (0, offset)
+
+
 class Gather:
     def __init__(self, here, wire, shard, full):
-        self.here, self.wire, self.shard, self.full = here, wire, shard, full
+        self.here, self.wire, self.shard = here, wire, shard
         self.core = []
+
+        def spot(number, y, b):
+            return full.at[here.y ^ y, here.a ^ number, here.b ^ b, here.c]
+
+        self.sheet = Sheet(here, wire, spot)
 
     @staticmethod
     def copies(dp, chain, mid):
         return (chain - 1) + (dp * mid - 1) * chain + dp * chain * mid
 
-    def spread(self, source, slot):
-        h = self.here
-        made = {
-            (y, b): self.wire.push(source, slot, h.to(y=y, b=b)) for y, b in h.plane()
-        }
-        self.core.append(self.wire.push(source, slot, h.to(c=1)))
-        return made
+    def landed(self, slot):
+        self.core.append(self.wire.push(slot, slot, self.here.to(c=1)))
 
     def start(self):
         h = self.here
-        slot = self.full.at[h.y, h.a, h.b, h.c]
+        slot = self.sheet.spot(0, 0, 0)
         self.chain = {
             o: self.wire.push(self.shard, slot, h.to(a=o)) for o in range(1, h.chain)
         }
-        self.sheet = {0: self.spread(self.shard, slot)}
+        self.sheet.start(0, self.shard)
+        self.core.append(self.wire.push(self.shard, slot, h.to(c=1)))
 
     def relay_chain(self):
-        h = self.here
-        for o in range(1, h.chain):
+        for o in range(1, self.here.chain):
             self.chain[o].wait_recv()
-            slot = self.full.at[h.y, h.a ^ o, h.b, h.c]
-            self.sheet[o] = self.spread(slot, slot)
+            slot = self.sheet.spot(o, 0, 0)
+            self.sheet.start(o, slot)
+            self.landed(slot)
 
     def relay_plane(self):
-        h = self.here
-        for o in range(h.chain):
-            for y, b in h.plane():
-                self.sheet[o][y, b].wait_recv()
-                slot = self.full.at[h.y ^ y, h.a ^ o, h.b ^ b, h.c]
-                self.core.append(self.wire.push(slot, slot, h.to(c=1)))
+        for o in range(self.here.chain):
+            self.sheet.relay(o, self.landed)
 
     def finish(self):
+        for o in range(self.here.chain):
+            self.sheet.finish(o, self.landed)
         for copy in self.core:
             copy.wait_recv()
 
 
-def call(body, outs, ins, scratch, ident, out_specs, in_specs, sent=0):
+class Line:
+    def __init__(self, here, block, full, sems):
+        self.here, self.block, self.full = here, block, full
+        self.send, self.recv, self.csend, self.crecv = sems
+
+    @staticmethod
+    def scratch(chain):
+        return [pltpu.SemaphoreType.DMA((n,)) for n in (2 * chain, chain, chain, chain)]
+
+    def along(self, source, owner, target, number):
+        return pltpu.make_async_remote_copy(
+            src_ref=source,
+            dst_ref=self.full.at[owner, self.here.c],
+            send_sem=self.send.at[number],
+            recv_sem=self.recv.at[owner],
+            device_id={"a": target},
+            device_id_type=pl.DeviceIdType.MESH,
+        )
+
+    def across(self, source, owner):
+        return pltpu.make_async_remote_copy(
+            src_ref=source,
+            dst_ref=self.full.at[owner, self.here.c],
+            send_sem=self.csend.at[owner],
+            recv_sem=self.crecv.at[owner],
+            device_id=self.here.to(c=1),
+            device_id_type=pl.DeviceIdType.MESH,
+        )
+
+    def start(self):
+        h = self.here
+
+        @pl.when(h.a < h.chain - 1)
+        def _():
+            self.along(self.block, h.a, h.a + 1, 0).start()
+
+        @pl.when(h.a > 0)
+        def _():
+            self.along(self.block, h.a, h.a - 1, 1).start()
+
+        self.across(self.block, h.a).start()
+
+    def step(self, s):
+        h = self.here
+
+        @pl.when(h.a - s >= 0)
+        def _():
+            owner = h.a - s
+            spot = self.full.at[owner, h.c]
+            self.along(spot, owner, h.a, 0).wait_recv()
+
+            @pl.when(h.a < h.chain - 1)
+            def _():
+                self.along(spot, owner, h.a + 1, 2 * s).start()
+
+            self.across(spot, owner).start()
+
+        @pl.when(h.a + s < h.chain)
+        def _():
+            owner = h.a + s
+            spot = self.full.at[owner, h.c]
+            self.along(spot, owner, h.a, 0).wait_recv()
+
+            @pl.when(h.a > 0)
+            def _():
+                self.along(spot, owner, h.a - 1, 2 * s + 1).start()
+
+            self.across(spot, owner).start()
+
+    def finish(self):
+        h = self.here
+        for s in range(h.chain):
+
+            @pl.when((h.a - s >= 0) & (h.a < h.chain - 1))
+            def _():
+                self.along(self.block, h.a, h.a, 2 * s).wait_send()
+
+            @pl.when((h.a + s < h.chain) & (h.a > 0))
+            def _():
+                self.along(self.block, h.a, h.a, 2 * s + 1).wait_send()
+
+        for owner in range(h.chain):
+            self.across(self.block, owner).wait_recv()
+            self.across(self.block, owner).wait_send()
+
+
+def call(body, outs, ins, scratch, ident, out_specs, in_specs, aliases=()):
     return pl.pallas_call(
         body,
         out_shape=outs,
         in_specs=in_specs,
         out_specs=out_specs,
         scratch_shapes=scratch,
+        input_output_aliases=dict(aliases),
         compiler_params=pltpu.CompilerParams(collective_id=ident, has_side_effects=True),
-        cost_estimate=pl.CostEstimate(flops=0, bytes_accessed=sent, transcendentals=0),
     )(*ins)
 
 
@@ -235,16 +366,24 @@
     return jnp.where(key_pos <= query_pos, values, 0.0)
 
 
+def expand_sheet(here, wire, ex_out):
+    def spot(number, y, b):
+        return ex_out.at[here.y ^ y, number, here.b ^ b]
+
+    return Sheet(here, wire, spot)
+
+
+EARLY = 3
+
+
 def second_kernel(
-    q_ref, kv_ref, wout_ref, cot_ref, o_ref, lse_ref, kv_out, wout_out, cot_out,
-    kv_all, send, recv, local,
+    q_ref, kv_ref, wout_ref, cot_ref, e1_ref,
+    o_ref, lse_ref, kv_out, wout_out, cot_out, ex_out,
+    kv_all, send, recv, lsend, lrecv, lcsend, lcrecv, local,
 ):
     h = Here()
     span = kv_ref.shape[1]
-    greet(
-        h,
-        chain_offsets(h) + plane_offsets(h) + [dict(c=1)],
-    )
+    greet(h, chain_offsets(h) + plane_offsets(h) + [dict(c=1)])
     wire = Wire(send, recv)
     own_out = pltpu.make_async_copy(wout_ref, wout_out.at[h.y, h.a, h.b, h.c], local.at[0])
     own_out.start()
@@ -261,21 +400,27 @@
     side = {(0, b): wire.push(kv_ref, mine, h.to(b=b)) for b in range(1, h.mid)}
     core.append(wire.push(kv_ref, mine, h.to(c=1)))
     gather = Gather(h, wire, wout_ref, wout_out)
+    gather.start()
+    cots = Line(h, cot_ref, cot_out, (lsend, lrecv, lcsend, lcrecv))
+    cots.start()
     for o in range(1, h.chain):
         chain[o].wait_recv()
         spot = block(o, 0, 0)
         for b in range(1, h.mid):
             side[o, b] = wire.push(spot, spot, h.to(b=b))
         core.append(wire.push(spot, spot, h.to(c=1)))
-    gather.start()
-    cots = {o: wire.push(cot_ref, cot_out.at[h.a, h.c], h.to(a=o)) for o in range(1, h.chain)}
-    cot_core = [wire.push(cot_ref, cot_out.at[h.a, h.c], h.to(c=1))]
+    sheet = expand_sheet(h, wire, ex_out)
+    kept = []
+    for a in range(EARLY):
+        sheet.start(a, e1_ref.at[a])
+        copy = pltpu.make_async_copy(e1_ref.at[a], ex_out.at[h.y, a, h.b], local.at[3 + a])
+        copy.start()
+        kept.append(copy)
     for o in range(h.chain):
         for b in range(1, h.mid):
             side[o, b].wait_recv()
             spot = block(o, b, 0)
             core.append(wire.push(spot, spot, h.to(c=1)))
-    gather.relay_chain()
     for copy in core:
         copy.wait_recv()
     store = pltpu.make_async_copy(kv_all, kv_out, local.at[2])
@@ -309,28 +454,37 @@
         lse_ref[g] = jnp.log(lse_ref[g])
         return unused
 
-    lax.fori_loop(0, KV_HEADS, head, 0)
+    lax.fori_loop(0, 2, head, 0)
+    gather.relay_chain()
+    cots.step(1)
+    lax.fori_loop(2, 4, head, 0)
+    sheet.relay(0)
+    cots.step(2)
+    lax.fori_loop(4, KV_HEADS, head, 0)
+    for a in range(1, EARLY):
+        sheet.relay(a)
     gather.relay_plane()
-    for o in range(1, h.chain):
-        cots[o].wait_recv()
-        spot = cot_out.at[h.a ^ o, h.c]
-        cot_core.append(wire.push(spot, spot, h.to(c=1)))
+    cots.step(3)
     gather.finish()
-    for copy in cot_core:
-        copy.wait_recv()
+    for a in range(EARLY):
+        sheet.finish(a)
+    cots.finish()
     wire.drain()
     own_out.wait()
     own_cot.wait()
     store.wait()
-
-
-def attend_forward(query, kv, wout, cot, sizes):
+    for copy in kept:
+        copy.wait()
+
+
+def attend_forward(query, kv, wout, cot, e1, sizes):
     dp, chain, mid, cores = sizes
+    assert chain == CHAIN
     blocks = chain * mid * cores
     rows = query.shape[1]
     count = (
         (chain - 1) + (mid - 1) * chain + chain * mid
-        + Gather.copies(dp, chain, mid) + 2 * (chain - 1) + 1
+        + Gather.copies(dp, chain, mid) + EARLY * (dp * mid - 1)
     )
     return call(
         second_kernel,
@@ -340,27 +494,34 @@
             jax.ShapeDtypeStruct((blocks,) + kv.shape, BF),
             jax.ShapeDtypeStruct((dp, chain, mid, cores) + wout.shape, BF),
             jax.ShapeDtypeStruct((chain, cores) + cot.shape, BF),
+            jax.ShapeDtypeStruct((dp, chain, mid) + e1.shape[1:], BF),
         ),
-        (query, kv, wout, cot),
-        [pltpu.VMEM((blocks,) + kv.shape, BF)] + wires(count) + [pltpu.SemaphoreType.DMA((3,))],
+        (query, kv, wout, cot, e1),
+        [pltpu.VMEM((blocks,) + kv.shape, BF)]
+        + wires(count)
+        + Line.scratch(chain)
+        + [pltpu.SemaphoreType.DMA((3 + EARLY,))],
         2,
-        (VMEM, VMEM, ANY, ANY, ANY),
-        [VMEM, VMEM, ANY, ANY],
-    )
-
-
-def third_kernel(n_ref, e1_ref, rd_ref, n_out, ex_out, rd_out, send, recv, rsend, rrecv, local):
+        (VMEM, VMEM, ANY, ANY, ANY, ANY),
+        [VMEM, VMEM, ANY, ANY, ANY],
+    )
+
+
+def third_kernel(
+    n_ref, e1_ref, rd_ref, ex_ref, n_out, rd_out, ex_out,
+    send, recv, rsend, rrecv, lsend, lrecv, lcsend, lcrecv, local,
+):
     h = Here()
     greet(h, chain_offsets(h) + block_offsets(h))
     wire = Wire(send, recv)
+    rows = Line(h, n_ref, n_out, (lsend, lrecv, lcsend, lcrecv))
+    rows.start()
     own = pltpu.make_async_copy(n_ref, n_out.at[h.a, h.c], local.at[0])
     own.start()
-    rows = {o: wire.push(n_ref, n_out.at[h.a, h.c], h.to(a=o)) for o in range(1, h.chain)}
-    core = [wire.push(n_ref, n_out.at[h.a, h.c], h.to(c=1))]
-    kept, sheets = [], []
-    for a in range(h.chain):
-        for y, b in h.plane():
-            sheets.append(wire.push(e1_ref.at[a], ex_out.at[h.y, a, h.b], h.to(y=y, b=b)))
+    sheet = expand_sheet(h, wire, ex_out)
+    kept = []
+    for a in range(EARLY, h.chain):
+        sheet.start(a, e1_ref.at[a])
         copy = pltpu.make_async_copy(e1_ref.at[a], ex_out.at[h.y, a, h.b], local.at[1 + a])
         copy.start()
         kept.append(copy)
@@ -390,18 +551,18 @@
     def _():
         reduce_copy(0, 0, 0).start()
 
-    for o in range(1, h.chain):
-        rows[o].wait_recv()
-        spot = n_out.at[h.a ^ o, h.c]
-        core.append(wire.push(spot, spot, h.to(c=1)))
-    for copy in core:
-        copy.wait_recv()
-    for copy in sheets:
-        copy.wait_recv()
+    rows.step(1)
+    for a in range(EARLY, h.chain):
+        sheet.relay(a)
+    for s in range(2, h.chain):
+        rows.step(s)
+    for a in range(EARLY, h.chain):
+        sheet.finish(a)
     for b in range(h.mid):
         for c in range(h.cores):
             spot = rd_out.at[b, c]
             pltpu.make_async_copy(spot, spot, rrecv.at[b * h.cores + c]).wait()
+    rows.finish()
     wire.drain()
     for copy in far:
         copy.wait_send()
@@ -415,30 +576,32 @@
         copy.wait()
 
 
-def gather_feed(normed, e1, rd, sizes):
+def gather_feed(normed, e1, rd, ex, sizes):
     dp, chain, mid, cores = sizes
-    count = 2 * (chain - 1) + 1 + chain * (dp * mid - 1)
+    count = (chain - EARLY) * (dp * mid - 1)
     return call(
         third_kernel,
         (
             jax.ShapeDtypeStruct((chain, cores) + normed.shape, BF),
-            jax.ShapeDtypeStruct((dp, chain, mid) + e1.shape[1:], BF),
             jax.ShapeDtypeStruct((mid, cores) + rd.shape, BF),
+            jax.ShapeDtypeStruct(ex.shape, BF),
         ),
-        (normed, e1, rd),
+        (normed, e1, rd, ex),
         wires(count)
         + [pltpu.SemaphoreType.DMA((dp * mid,)), pltpu.SemaphoreType.DMA((mid * cores,))]
+        + Line.scratch(chain)
         + [pltpu.SemaphoreType.DMA((1 + chain,))],
         3,
         (ANY, ANY, ANY),
-        [ANY, ANY, ANY],
+        [ANY, ANY, ANY, ANY],
+        aliases={3: 2},
     )
 
 
 class Fold:
-    def __init__(self, here, wire, part, near, half, far):
+    def __init__(self, here, wire, part, near, far):
         self.here, self.wire, self.part = here, wire, part
-        self.near, self.half, self.far = near, half, far
+        self.near, self.far = near, far
 
     @staticmethod
     def copies(chain):
@@ -447,7 +610,7 @@
     @staticmethod
     def scratch(part):
         chain, cores, rows, width = part.shape
-        return [pltpu.VMEM((chain, rows, width), BF) for _ in range(3)]
+        return [pltpu.VMEM((chain, rows, width), BF) for _ in range(2)]
 
     def start(self):
         h = self.here
@@ -466,11 +629,11 @@
             def add(i, unused):
                 at = pl.ds(pl.multiple_of(i * 16, 16), 16)
                 both = self.part[h.a ^ o, h.c, at].astype(F32) + self.near[o, at].astype(F32)
-                self.half[o, at] = both.astype(BF)
+                self.near[o, at] = both.astype(BF)
                 return unused
 
             lax.fori_loop(0, rows // 16, add, 0)
-            self.sent[o] = self.wire.push(self.half.at[o], self.far.at[o], h.to(a=o))
+            self.sent[o] = self.wire.push(self.near.at[o], self.far.at[o], h.to(a=o))
         self.swap[0].wait_recv()
 
     def finish(self, out):
@@ -494,11 +657,22 @@
     return chain_offsets(here) + [dict(c=1)]
 
 
-def fourth_kernel(part_ref, gr_ref, out_ref, gr_out, near, half, far, send, recv, gsend, grecv):
+def push_expand(here, wire, ge_ref, ge_out, first, count):
+    made = []
+    for a in range(first, first + count):
+        for i, (y, b) in enumerate(here.plane()):
+            source = ge_ref.at[here.y ^ y, a, here.b ^ b]
+            made.append(wire.push(source, ge_out.at[i, a - first], here.to(y=y, b=b)))
+    return made
+
+
+def fourth_kernel(
+    part_ref, gr_ref, ge_ref, out_ref, gr_out, ge_out, near, far, send, recv, gsend, grecv
+):
     h = Here()
     greet(h, chain_offsets(h) + block_offsets(h))
     wire = Wire(send, recv)
-    fold = Fold(h, wire, part_ref, near, half, far)
+    fold = Fold(h, wire, part_ref, near, far)
     fold.start()
     slot = h.y * h.mid + h.b
 
@@ -526,8 +700,11 @@
     def _():
         chunk_copy(0, 0).start()
 
+    sheets = push_expand(h, wire, ge_ref, ge_out, 0, AHEAD)
     fold.pass_on()
     fold.finish(out_ref)
+    for copy in sheets:
+        copy.wait_recv()
     for i in range(h.dp * h.mid):
         pltpu.make_async_copy(gr_out.at[i], gr_out.at[i], grecv.at[i]).wait()
     wire.drain()
@@ -539,197 +716,79 @@
         chunk_copy(0, 0).wait_send()
 
 
-def fold_feed(part, gr, sizes):
+AHEAD = 1
+
+
+def fold_feed(part, gr, ge, sizes):
     dp, chain, mid, cores = sizes
+    others = dp * mid - 1
     return call(
         fourth_kernel,
         (
             jax.ShapeDtypeStruct(part.shape[2:], F32),
             jax.ShapeDtypeStruct((dp * mid,) + gr.shape[2:], BF),
+            jax.ShapeDtypeStruct((others, AHEAD) + ge.shape[3:], BF),
         ),
-        (part, gr),
+        (part, gr, ge),
         Fold.scratch(part)
-        + wires(Fold.copies(chain))
+        + wires(Fold.copies(chain) + others * AHEAD)
         + [pltpu.SemaphoreType.DMA((mid * cores,)), pltpu.SemaphoreType.DMA((dp * mid,))],
         4,
-        (VMEM, ANY),
-        [VMEM, ANY],
-    )
-
-
-def fifth_kernel(
-    q_ref, do_ref, lse_ref, delta_ref, kv_ref, part_ref, ge_ref,
-    dq_ref, dkv_ref, out_ref, ge_out,
-    made, got, near, half, far, send, recv, ksend, krecv,
-):
-    h = Here()
-    span = kv_ref.shape[2]
-    blocks = kv_ref.shape[0]
-    greet(
-        h,
-        [
-            dict(a=a, b=b, c=c)
-            for a in range(h.chain)
-            for b in range(h.mid)
-            for c in range(h.cores)
-            if a or b or c
-        ]
-        + [dict(y=y, b=b) for y, b in h.plane() if y],
-    )
-    wire = Wire(send, recv)
-    fold = Fold(h, wire, part_ref, near, half, far)
-    fold.start()
-    sheets = []
-    for i, (y, b) in enumerate(h.plane()):
-        for a in range(h.chain):
-            sheets.append(
-                wire.push(ge_ref.at[h.y ^ y, a, h.b ^ b], ge_out.at[i, a], h.to(y=y, b=b))
-            )
-    fold.pass_on()
-
-    last = h.rank // 2
-
-    def visit(pair, hide):
-        def head(g, unused):
-            query, dout = q_ref[g], do_ref[g]
-            keys = kv_ref[pl.ds(2 * pair, 2), g].reshape(2 * span, WIDE)
-            probs = jnp.exp(mm(keys, query, NT) - lse_ref[g])
-            if hide:
-                probs = masked(probs, pair, h.rank, span)
-            slope = probs * (mm(keys, dout, NT) - delta_ref[g])
-            slope = slope.astype(BF)
-            both = mm(slope, query, NN) + mm(probs.astype(BF), dout, NN)
-            made[pl.ds(2 * pair, 2), g] = both.astype(BF).reshape(2, span, WIDE)
-            add = mm(keys, slope, TN)[:HD]
-            if hide:
-                dq_ref[g] = add
-            else:
-                dq_ref[g] += add
-            return unused
-
-        lax.fori_loop(0, KV_HEADS, head, 0)
-
-    def block_copy(o):
-        peer = h.rank ^ o
-        c, b, a = o % h.cores, (o // h.cores) % h.mid, o // (h.cores * h.mid)
-        return pltpu.make_async_remote_copy(
-            src_ref=made.at[peer],
-            dst_ref=got.at[o],
-            send_sem=ksend.at[o],
-            recv_sem=krecv.at[o],
-            device_id=h.to(a=a, b=b, c=c),
-            device_id_type=pl.DeviceIdType.MESH,
-        )
-
-    visit(last, True)
-
-    def step(pair, unused):
-        visit(pair, False)
-        return unused
-
-    lax.fori_loop(0, last, step, 0)
-    for o in range(1, blocks):
-
-        @pl.when((h.rank ^ o) < h.rank)
-        def _():
-            block_copy(o).start()
-
-    fold.finish(out_ref)
-    dkv_ref[...] = made[h.rank].astype(F32)
-    for o in range(1, blocks):
-
-        @pl.when((h.rank ^ o) > h.rank)
-        def _():
-            block_copy(o).wait_recv()
-            dkv_ref[...] += got[o].astype(F32)
-
-        @pl.when((h.rank ^ o) < h.rank)
-        def _():
-            block_copy(o).wait_send()
-
-    for copy in sheets:
-        copy.wait_recv()
-    wire.drain()
-
-
-def attend_backward(query, dout, lse, delta, kv, part, ge, sizes):
-    dp, chain, mid, cores = sizes
-    blocks = chain * mid * cores
-    rows = query.shape[1]
-    others = dp * mid - 1
-    return call(
-        fifth_kernel,
-        (
-            jax.ShapeDtypeStruct((KV_HEADS, HD, rows), F32),
-            jax.ShapeDtypeStruct(kv.shape[1:], F32),
-            jax.ShapeDtypeStruct(part.shape[2:], F32),
-            jax.ShapeDtypeStruct((others, chain) + ge.shape[3:], BF),
-        ),
-        (query, dout, lse, delta, kv, part, ge),
-        [pltpu.VMEM(kv.shape, BF), pltpu.VMEM(kv.shape, BF)]
-        + Fold.scratch(part)
-        + wires(Fold.copies(chain) + others * chain)
-        + wires(blocks),
-        5,
-        (VMEM, VMEM, VMEM, ANY),
-        [VMEM, VMEM, VMEM, VMEM, VMEM, VMEM, ANY],
+        (VMEM, ANY, ANY),
+        [VMEM, ANY, ANY],
     )
 
 
 class Scatter:
-    def __init__(self, here, wire, grad, out, near, half, sheet, line, far, columns):
-        self.here, self.wire, self.grad, self.out = here, wire, grad, out
-        self.near, self.half, self.sheet, self.line, self.far = near, half, sheet, line, far
-        self.columns = columns
+    def __init__(self, here, wire, pick, spots, out, bufs, columns):
+        self.here, self.wire, self.pick, self.out = here, wire, pick, out
+        self.near, self.sheet, self.line, self.far = bufs
+        self.spots, self.columns = spots + [(0, 0)], columns
 
     @staticmethod
-    def copies(dp, chain, mid):
-        return dp * mid + (dp * mid - 1) + (chain - 1)
+    def copies(spots, chain):
+        return (spots + 1) + spots + (chain - 1)
 
     @staticmethod
-    def scratch(grad):
-        dp, chain, mid, cores, rows, width = grad.shape
+    def scratch(spots, chain, rows, width):
         return [
-            pltpu.VMEM((dp * mid, chain, rows, width), BF),
-            pltpu.VMEM((dp * mid, chain, rows, width), BF),
-            pltpu.VMEM((dp * mid, chain, rows, width), BF),
+            pltpu.VMEM((spots + 1, chain, rows, width), BF),
+            pltpu.VMEM((spots, chain, rows, width), BF),
             pltpu.VMEM((chain, rows, width), BF),
             pltpu.VMEM((chain, rows, width), BF),
         ]
 
-    def order(self):
-        return self.here.plane() + [(0, 0)]
-
     def start(self):
         h = self.here
         self.swap = [
             self.wire.push(
-                self.grad.at[h.y ^ y, :, h.b ^ b, h.c ^ 1, :, self.columns],
+                self.pick(h.y ^ y, h.b ^ b, h.c ^ 1).at[:, :, self.columns],
                 self.near.at[i, :, :, self.columns],
                 h.to(c=1),
             )
-            for i, (y, b) in enumerate(self.order())
+            for i, (y, b) in enumerate(self.spots)
         ]
 
     def over_plane(self):
         h = self.here
         self.sent = []
-        for i, (y, b) in enumerate(self.order()):
+        for i, (y, b) in enumerate(self.spots):
             self.swap[i].wait_recv()
+            mine = self.pick(h.y ^ y, h.b ^ b, h.c)
 
             def add(a, unused):
                 total = (
-                    self.grad[h.y ^ y, a, h.b ^ b, h.c, :, self.columns].astype(F32)
+                    mine[a, :, self.columns].astype(F32)
                     + self.near[i, a, :, self.columns].astype(F32)
                 )
-                self.half[i, a, :, self.columns] = total.astype(BF)
+                self.near[i, a, :, self.columns] = total.astype(BF)
                 return unused
 
             lax.fori_loop(0, h.chain, add, 0)
             if y or b:
                 self.sent.append(
                     self.wire.push(
-                        self.half.at[i, :, :, self.columns],
+                        self.near.at[i, :, :, self.columns],
                         self.sheet.at[i, :, :, self.columns],
                         h.to(y=y, b=b),
                     )
@@ -737,12 +796,12 @@
 
     def over_chain(self):
         h = self.here
-        own = len(self.order()) - 1
+        own = len(self.spots) - 1
         for copy in self.sent:
             copy.wait_recv()
         self.last = []
         for o in list(range(1, h.chain)) + [0]:
-            total = self.half[own, h.a ^ o, :, self.columns].astype(F32)
+            total = self.near[own, h.a ^ o, :, self.columns].astype(F32)
             for i in range(own):
                 total = total + self.sheet[i, h.a ^ o, :, self.columns].astype(F32)
             if o:
@@ -767,22 +826,149 @@
         self.out[:, self.columns] = total
 
 
-def sixth_kernel(
-    gi_ref, go_ref, ge_ref, gi_out, go_out, ge_out,
-    n1, h1, s1, l1, f1, n2, h2, s2, l2, f2, send, recv, local,
+def fifth_kernel(
+    q_ref, do_ref, lse_ref, delta_ref, kv_ref, part_ref, go_ref, ge_ref,
+    dq_ref, dkv_ref, out_ref, go_out, ge_out, made, *rest,
 ):
+    k_bufs, w_bufs, f_bufs, (send, recv, local) = rest[:4], rest[4:8], rest[8:10], rest[10:]
     h = Here()
-    greet(
-        h,
-        [dict(a=a, c=c) for a in range(h.chain) for c in range(h.cores) if a or c]
-        + plane_offsets(h),
-    )
+    span = kv_ref.shape[-2] // KV_HEADS
+    load = pltpu.make_async_copy(kv_ref, made, local)
+    load.start()
+    greet(h, chain_offsets(h) + plane_offsets(h) + [dict(c=1)])
+    wire = Wire(send, recv)
+    fold = Fold(h, wire, part_ref, *f_bufs)
+    fold.start()
+
+    def weight_pick(y, b, c):
+        return go_ref.at[y, :, b, c]
+
+    weights = Scatter(
+        h, wire, weight_pick, h.plane(), go_out, w_bufs, pl.ds(0, go_ref.shape[-1])
+    )
+    weights.start()
+    fold.pass_on()
+    weights.over_plane()
+    sheets = push_expand(h, wire, ge_ref, ge_out.at[:, 0:1], AHEAD, 1)
+
+    last = h.rank // 2
+
+    def visit(pair, hide):
+        def head(g, unused):
+            query, dout = q_ref[g], do_ref[g]
+            rows = pl.ds(pl.multiple_of(g * span, span), span)
+            spot = (pair // h.mid, lax.rem(pair, h.mid), slice(None), rows)
+            keys = made[spot].reshape(2 * span, WIDE)
+            probs = jnp.exp(mm(keys, query, NT) - lse_ref[g])
+            if hide:
+                probs = masked(probs, pair, h.rank, span)
+            slope = probs * (mm(keys, dout, NT) - delta_ref[g])
+            slope = slope.astype(BF)
+            both = mm(slope, query, NN) + mm(probs.astype(BF), dout, NN)
+            made[spot] = both.astype(BF).reshape(2, span, WIDE)
+            add = mm(keys, slope, TN)[:HD]
+            if hide:
+                dq_ref[g] = add
+            else:
+                dq_ref[g] += add
+            return unused
+
+        lax.fori_loop(0, KV_HEADS, head, 0)
+
+    load.wait()
+    visit(last, True)
+
+    def step(pair, unused):
+        visit(pair, False)
+        return unused
+
+    lax.fori_loop(0, last, step, 0)
+
+    def clear(pair, unused):
+        made[pair // h.mid, lax.rem(pair, h.mid)] = jnp.zeros(made.shape[2:], BF)
+        return unused
+
+    lax.fori_loop(last + 1, h.chain * h.mid, clear, 0)
+
+    def key_pick(y, b, c):
+        return made.at[:, b, c]
+
+    keys_fold = Scatter(
+        h, wire, key_pick, [(0, b) for b in range(1, h.mid)], dkv_ref, k_bufs, pl.ds(0, WIDE)
+    )
+    keys_fold.start()
+    keys_fold.over_plane()
+    sheets += push_expand(h, wire, ge_ref, ge_out.at[:, 1:], AHEAD + 1, h.chain - AHEAD - 1)
+    weights.over_chain()
+    fold.finish(out_ref)
+    keys_fold.over_chain()
+    weights.finish()
+    keys_fold.finish()
+    for copy in sheets:
+        copy.wait_recv()
+    wire.drain()
+
+
+def attend_backward(query, dout, lse, delta, kv, part, go, ge, sizes):
+    dp, chain, mid, cores = sizes
+    rows = query.shape[1]
+    span = kv.shape[2]
+    kv = kv.reshape(chain, mid, cores, KV_HEADS * span, WIDE)
+    others = dp * mid - 1
+    count = (
+        Fold.copies(chain)
+        + Scatter.copies(others, chain)
+        + Scatter.copies(mid - 1, chain)
+        + others * (chain - AHEAD)
+    )
+    return call(
+        fifth_kernel,
+        (
+            jax.ShapeDtypeStruct((KV_HEADS, HD, rows), F32),
+            jax.ShapeDtypeStruct((KV_HEADS * span, WIDE), F32),
+            jax.ShapeDtypeStruct(part.shape[2:], F32),
+            jax.ShapeDtypeStruct(go.shape[4:], F32),
+            jax.ShapeDtypeStruct((others, chain - AHEAD) + ge.shape[3:], BF),
+        ),
+        (query, dout, lse, delta, kv, part, go, ge),
+        [pltpu.VMEM((chain, mid, cores, KV_HEADS * span, WIDE), BF)]
+        + Scatter.scratch(mid - 1, chain, KV_HEADS * span, WIDE)
+        + Scatter.scratch(others, chain, *go.shape[4:])
+        + Fold.scratch(part)
+        + wires(count)
+        + [pltpu.SemaphoreType.DMA],
+        5,
+        (VMEM, VMEM, VMEM, VMEM, ANY),
+        [VMEM, VMEM, VMEM, VMEM, ANY, VMEM, VMEM, ANY],
+    )
+
+
+def all_offsets(here):
+    return [
+        dict(y=y, a=a, b=b, c=c)
+        for y in range(here.dp)
+        for a in range(here.chain)
+        for b in range(here.mid)
+        for c in range(here.cores)
+        if y or a or b or c
+    ]
+
+
+def sixth_kernel(gi_ref, ge_ref, x_ref, gi_out, ge_out, total_ref, *rest):
+    bufs, (vector, got, send, recv, local) = rest[:4], rest[4:]
+    h = Here()
+    greet(h, all_offsets(h))
     wire = Wire(send, recv)
     width = FF // (h.chain * h.cores)
+    half_width = gi_ref.shape[-1] // 2
+
+    def pick(y, b, c):
+        return gi_ref.at[y, :, b, c]
+
     jobs = [
-        Scatter(h, wire, gi_ref, gi_out, n1, h1, s1, l1, f1, columns)
-        for columns in (pl.ds(0, gi_ref.shape[-1] // 2), pl.ds(gi_ref.shape[-1] // 2, gi_ref.shape[-1] // 2))
-    ] + [Scatter(h, wire, go_ref, go_out, n2, h2, s2, l2, f2, pl.ds(0, go_ref.shape[-1]))]
+        Scatter(h, wire, pick, h.plane(), gi_out, bufs, pl.ds(i * half_width, half_width))
+        for i in range(2)
+    ]
     for job in jobs:
         job.start()
     kept, swaps = [], []
@@ -798,71 +984,47 @@
                     copy = pltpu.make_async_copy(source, spot, local.at[part])
                     copy.start()
                     kept.append(copy)
-    jobs[0].over_plane()
-    jobs[1].over_plane()
-    jobs[2].over_plane()
+    for job in jobs:
+        job.over_plane()
     for job in jobs:
         job.over_chain()
     for job in jobs:
         job.finish()
+    squares = jnp.sum(gi_out[...] * gi_out[...])
+    last = lax.broadcasted_iota(jnp.int32, x_ref.shape, 0) == x_ref.shape[0] - 1
+    vector[...] = x_ref[...] + jnp.where(last, squares, 0.0)
+    small = [wire.push(vector, got.at[h.shard], h.to(**offset)) for offset in all_offsets(h)]
+    got[h.shard] = vector[...]
     for copy in swaps:
         copy.wait_recv()
+    for copy in small:
+        copy.wait_recv()
+    total_ref[...] = jnp.sum(got[...], axis=0)
     wire.drain()
     for copy in kept:
         copy.wait()
 
 
-def scatter_projections(gi, go, ge, sizes):
+def scatter_projections(gi, ge, x, sizes):
     dp, chain, mid, cores = sizes
-    count = 3 * Scatter.copies(dp, chain, mid) + 2 * (chain * cores - 1)
+    others = dp * mid - 1
+    devices = math.prod(sizes)
+    count = 2 * Scatter.copies(others, chain) + 2 * (chain * cores - 1) + devices - 1
     return call(
         sixth_kernel,
         (
             jax.ShapeDtypeStruct(gi.shape[4:], F32),
-            jax.ShapeDtypeStruct(go.shape[4:], F32),
             jax.ShapeDtypeStruct((ge.shape[2], 2 * FF), BF),
+            jax.ShapeDtypeStruct(x.shape, F32),
         ),
-        (gi, go, ge),
-        Scatter.scratch(gi)
-        + Scatter.scratch(go)
+        (gi, ge, x),
+        Scatter.scratch(others, chain, *gi.shape[4:])
+        + [pltpu.VMEM(x.shape, F32), pltpu.VMEM((devices,) + x.shape, F32)]
         + wires(count)
         + [pltpu.SemaphoreType.DMA((2,))],
         6,
-        (VMEM, VMEM, ANY),
-        [VMEM, VMEM, ANY],
-    )
-
-
-def seventh_kernel(x_ref, out_ref, got, send, recv):
-    h = Here()
-    offsets = [
-        dict(y=y, a=a, b=b, c=c)
-        for y in range(h.dp)
-        for a in range(h.chain)
-        for b in range(h.mid)
-        for c in range(h.cores)
-        if y or a or b or c
-    ]
-    greet(h, offsets)
-    wire = Wire(send, recv)
-    copies = [wire.push(x_ref, got.at[h.shard], h.to(**offset)) for offset in offsets]
-    got[h.shard] = x_ref[...]
-    for copy in copies:
-        copy.wait_recv()
-    out_ref[...] = jnp.sum(got[...], axis=0)
-    wire.drain()
-
-
-def total_of(x, sizes):
-    count = math.prod(sizes)
-    return call(
-        seventh_kernel,
-        jax.ShapeDtypeStruct(x.shape, F32),
-        (x,),
-        [pltpu.VMEM((count,) + x.shape, F32)] + wires(count),
-        7,
-        VMEM,
-        [VMEM],
+        (VMEM, ANY, VMEM),
+        [VMEM, ANY, VMEM],
     )
 
 
@@ -947,8 +1109,8 @@
     query_wide = jnp.pad(query_low, ((0, 0), (0, 0), (0, HD)))
     kv_low = jnp.concatenate([key_rows, value_rows], axis=-1).astype(BF).transpose(1, 0, 2)
 
-    attended_cols, log_mass, kv_all, full_output, cot_all = attend_forward(
-        query_wide, kv_low, output_weight.astype(BF), upstream_low, sizes
+    attended_cols, log_mass, kv_all, full_output, cot_all, ex_part = attend_forward(
+        query_wide, kv_low, output_weight.astype(BF), upstream_low, e1, sizes
     )
     full_output = full_output.reshape(-1, model_width)
     attended = by_row(attended_cols, rows)
@@ -958,7 +1120,7 @@
     normed_two, norm_two_pull = jax.vjp(rms_normed, residual, norm_gains[1])
     normed_two = normed_two.astype(BF)
 
-    n_all, ex_all, rd_all = gather_feed(normed_two, e1, reduce_weight.astype(BF), sizes)
+    n_all, rd_all, ex_all = gather_feed(normed_two, e1, reduce_weight.astype(BF), ex_part, sizes)
     n_all = n_all.reshape(-1, model_width)
     cot_all = cot_all.reshape(-1, model_width)
     ex_all = ex_all.reshape(model_width, -1)
@@ -977,13 +1139,18 @@
     ).astype(BF)
     back_part = jnp.einsum("rf,df->rd", expand_grad, ex_all, preferred_element_type=F32).astype(BF)
     grad_reduce = jnp.einsum("rf,rd->fd", hidden, cot_all, preferred_element_type=F32).astype(BF)
-    normed_two_grad, reduce_got = fold_feed(
+    grad_expand = jnp.einsum("rd,rf->df", n_all, expand_grad, preferred_element_type=F32).astype(BF)
+    grad_expand = grad_expand.reshape(dp, chain, mid, cores, -1, grad_expand.shape[1])
+    normed_two_grad, reduce_got, expand_got = fold_feed(
         back_part.reshape(chain, cores, rows, model_width),
         grad_reduce.reshape(mid, cores, -1, model_width),
+        grad_expand,
         sizes,
     )
     out_part = jnp.dot(hidden, rd_all, preferred_element_type=F32).astype(BF)
-    grad_expand = jnp.einsum("rd,rf->df", n_all, expand_grad, preferred_element_type=F32).astype(BF)
+
+    def sharded(grad):
+        return grad.astype(BF).reshape(dp, chain, mid, cores, -1, grad.shape[1])
 
     residual_part, gain_two_grad = norm_two_pull(normed_two_grad)
     residual_grad = upstream_low.astype(F32) + residual_part
@@ -997,19 +1164,19 @@
     )
     row_delta = row_delta.transpose(1, 2, 0).reshape(KV_HEADS, 1, GROUP * rows)
     dout_wide = jnp.pad(by_group(attended_grad), ((0, 0), (0, 0), (HD, 0)))
-    grad_expand = grad_expand.reshape(dp, chain, mid, cores, -1, grad_expand.shape[1])
-    query_cols, kv_grad, result, expand_got = attend_backward(
+    query_cols, kv_grad, result, shard_output, expand_rest = attend_backward(
         query_wide,
         dout_wide,
         log_mass,
         row_delta,
         kv_all,
         out_part.reshape(chain, cores, rows, model_width),
+        sharded(grad_output),
         grad_expand,
         sizes,
     )
     query_grads = by_row(query_cols, rows) * score_scale
-    kv_grad = kv_grad.transpose(1, 0, 2)
+    kv_grad = kv_grad.reshape(KV_HEADS, rows, WIDE).transpose(1, 0, 2)
     projected_grad, head_grads = prepare_pull(
         (query_grads.reshape(rows, HEADS, HD), kv_grad[..., :HD], kv_grad[..., HD:])
     )
@@ -1025,37 +1192,30 @@
     y_here, b_here = lax.axis_index("dp"), lax.axis_index("b")
     own_expand = lax.dynamic_index_in_dim(grad_expand, y_here, 0, keepdims=False)
     own_expand = lax.dynamic_index_in_dim(own_expand, b_here, 1, keepdims=False)
+    expand_got = jnp.concatenate([expand_got, expand_rest], axis=1)
     sum_expand = own_expand.astype(F32) + jnp.sum(expand_got.astype(F32), axis=0)
+    sum_expand = sum_expand.astype(BF)
+    sum_wide = sum_expand.astype(F32)
     shard_reduce = jnp.sum(reduce_got.astype(F32), axis=0)
-
-    def sharded(grad):
-        return grad.astype(BF).reshape(dp, chain, mid, cores, -1, grad.shape[1])
-
-    shard_input, shard_output, shard_expand = scatter_projections(
-        sharded(grad_input), sharded(grad_output), sum_expand.astype(BF), sizes
-    )
-    shard_expand = shard_expand.astype(F32)
     squares_local = (
-        jnp.sum(shard_input * shard_input)
-        + jnp.sum(shard_output * shard_output)
-        + jnp.sum(shard_expand * shard_expand)
+        jnp.sum(shard_output * shard_output)
+        + jnp.sum(sum_wide * sum_wide)
         + jnp.sum(shard_reduce * shard_reduce)
     )
     gain_count = norm_gains.size
     head_count = head_gains.size
-    packed = jnp.concatenate(
-        [
-            gain_one_grad,
-            gain_two_grad,
-            head_grads.reshape(-1),
-            jnp.full((128,), squares_local, F32),
-        ]
-    ).reshape(-1, 128)
-    packed = jnp.pad(packed, ((0, -packed.shape[0] % 8), (0, 0)))
-    totals = total_of(packed, sizes).reshape(-1)
+    packed = jnp.concatenate([gain_one_grad, gain_two_grad, head_grads.reshape(-1)])
+    packed = packed.reshape(-1, 128)
+    packed = jnp.pad(packed, ((0, -(packed.shape[0] + 1) % 8), (0, 0)))
+    packed = jnp.concatenate([packed, jnp.full((1, 128), squares_local, F32)])
+    shard_input, shard_expand, totals = scatter_projections(
+        sharded(grad_input), sum_expand, packed, sizes
+    )
+    shard_expand = shard_expand.astype(F32)
+    square_total = totals[-1, 0]
+    totals = totals.reshape(-1)
     gain_totals = totals[:gain_count].reshape(norm_gains.shape)
     head_totals = totals[gain_count : gain_count + head_count].reshape(head_gains.shape)
-    square_total = totals[gain_count + head_count]
     grad_norm = jnp.sqrt(
         square_total + jnp.sum(gain_totals * gain_totals) + jnp.sum(head_totals * head_totals)
     )

time: 728 us -> 616 us (0.85)
  Pallas kernels: 558 us -> 454 us
    pallas_call x7 -> x6, Pallas kernels: 558 us -> 454 us  [call(): pl.pallas_call(body, out_shape=outs, in_specs=in_specs, out_specs=out_spe...]
where the time goes in v2:
time: 616 us; the launch traced here: 611 us
  Pallas kernels  454 us (74%)
  matrix products  70.9 us (12%)
  other arithmetic  54.2 us (9%)
  local copies, waits for them, and re-layouts  24.1 us (4%)
  between operations  7.64 us (1%)
    pallas_call x6, Pallas kernels, call(): pl.pallas_call(body, out_shape=outs, in_specs=in_specs, out_specs=out_spe...  454 us

profile of v2, /device:TPU:0, one launch (start us, length us, event | category | flops | bytes accessed | tf_op | source)
XLA Modules:
  0.0 610.9 jit_solution(27630200267264212)
XLA Ops:
  2.7 3.0 convert_element_type.135.ex_ref
  6.5 57.5 %shard_map.262 = (bf16[2,4,2,2,64,2304]{5,4,3,2,1,0:T(8,128)(2,1)}, bf16[4,2,64,1280]{3,2,1,0:T(8,128)(2,1)}) custom-call(bf16[64,2304]{1,0:T(8,128)(2,1)} %convert_element_type.134.win_ref, bf16[64,10240]{1,0:T(8,128)(2,1)} %convert_element_type.135.ex_ref), custom_call_target="tpu_custom_call" | custom-call | tf_op jit(solution)/shard_map/pallas_call | solution.py:291
  64.0 5.1 fusion.20
  77.9 88.2 %shard_map.263 = (f32[6,64,512]{2,1,0:T(8,128)}, f32[6,1,512]{2,1,0:T(1,128)}, bf16[16,6,128,128]{3,2,1,0:T(8,128)(2,1)}, bf16[2,4,2,2,48,2048]{5,4,3,2,1,0:T(8,...) custom-call(bf16[6,512,128]{2,1,0:T(8,128)(2,1)} %pad.40.q_ref, ...), custom_call_target="tpu_custom_call" | custom-call | tf_op jit(solution)/shard_map/pallas_call | solution.py:291
  167.3 4.0 multiply_reduce_fusion.4
  173.1 52.6 %shard_map.264 = (bf16[4,2,128,2048]{3,2,1,0:T(8,128)(2,1)}, bf16[2,2,160,2048]{3,2,1,0:T(8,128)(2,1)}, bf16[2,4,2,2,64,1280]{5,4,3,2,1,0:T(8,128)(2,1)}) custom-call(bf16[128,2048]{1,0:T(8,128)(2,1)} %multiply_convert_fusion.3.n_ref, bf16[4,2,64,1280]{3,2,1,0:T(8,128)(2,1)} %get-tuple-element.38.e1_ref, ...), custom_call_target="tpu_custom_call", output_to_operand_aliasing={{2}: (3, {})} | custom-call | tf_op jit(solution)/shard_map/pallas_call | solution.py:291
  225.8 9.2 %fusion.39 = f32[1024,1280]{0,1:T(8,128)S(1)} fusion(bf16[1024,2048]{1,0:T(8,128)(2,1)} %bitcast.188, bf16[2048,1280]{1,0:T(8,128)(2,1)} %bitcast.150), kind=kOutput, calls=%fused_computation.127 | convolution fusion | flops 5368709120 | bytes 14680064 | tf_op jit(solution)/shard_map/dot_general | solution.py:1129
  235.0 3.8 multiply_convert_fusion.2
  238.8 7.7 %convolution_convert_fusion.2 = bf16[2048,1280]{1,0:T(8,128)(2,1)} fusion(bf16[1024,2048]{1,0:T(8,128)(2,1)S(1)} %bitcast.189, bf16[1024,640]{0,1:T(8,128)(2,1)S(1)} %get-tuple-element.82, bf16[1024,640]{0,1:T(8,128)(2,1)S(1)} %get-tuple-element.81), kind=kOutput, calls=%fused_computation.3 | convolution fusion | flops 5376573440 | bytes 12058624 | tf_op jit(solution)/shard_map/rd,rf->df/dot_general | solution.py:1142
  246.6 4.2 convolution_convert_fusion.5
  250.7 7.2 %convolution_convert_fusion.4 = bf16[1024,2048]{1,0:T(8,128)(2,1)} fusion(bf16[2048,1280]{1,0:T(8,128)(2,1)S(1)} %bitcast.153, bf16[1024,640]{0,1:T(8,128)(2,1)S(1)} %get-tuple-element.82, bf16[1024,640]{0,1:T(8,128)(2,1)S(1)} %get-tuple-element.81), kind=kOutput, calls=%fused_computation.6 | convolution fusion | flops 5376049152 | bytes 12058624 | tf_op jit(solution)/shard_map/rf,df->rd/dot_general | solution.py:1140
  258.0 50.3 %shard_map.265 = (f32[128,2048]{1,0:T(8,128)}, bf16[4,160,2048]{2,1,0:T(8,128)(2,1)}, bf16[3,1,2,64,1280]{4,3,2,1,0:T(8,128)(2,1)}) custom-call(bf16[4,2,128,2048]{3,2,1,0:T(8,128)(2,1)} %bitcast.154, bf16[2,2,160,2048]{3,2,1,0:T(8,128)(2,1)} %bitcast.164, bf16[2,4,2,2,64,1280]{5,4,3,2,1,0:T(8,128)(2,1)} %bitcast.139), custom_call_target="tpu_custom_call" | custom-call | tf_op jit(solution)/shard_map/pallas_call | solution.py:291
  308.3 2.2 multiply_reduce_fusion.2
  312.1 4.4 convolution_convert_fusion.1
  316.5 5.5 convolution_convert_fusion.3
  322.0 2.3 copy.75
  324.3 6.2 %convert_multiply_fusion.1 = (f32[128,1536]{1,0:T(8,128)}, bf16[128,1536]{1,0:T(8,128)(2,1)}) fusion(f32[128,1536]{1,0:T(8,128)} %copy.75, bf16[1536,2048]{1,0:T(8,128)(2,1)} %bitcast.137, f32[128,2048]{1,0:T(8,128)S(1)} %fusion.14), kind=kOutput, calls=%fused_computation.58 | convolution fusion | flops 806158336 | bytes 9306112 | tf_op jit(solution)/shard_map/rd,hd->rh/dot_general | solution.py:1159
  332.3 2.2 copy.74
  334.5 2.3 pad.41.do_ref
  336.8 2.3 copy.76
  340.9 111.1 %shard_map.266 = (f32[6,64,512]{2,1,0:T(8,128)}, f32[768,128]{1,0:T(8,128)}, f32[128,2048]{1,0:T(8,128)}, f32[48,2048]{1,0:T(8,128)}, bf16[3,3,2,64,1280]{4,3,2,1,0:T(8,128)(2,1)}) custom-call(bf16[6,512,128]{2,1,0:T(8,128)(2,1)} %pad.40.q_ref, bf16[6,512,128]{2,1,0:T(8,128)(2,1)} %pad.41.do_ref, f32[6,1,512]{2,1,0:T(1,128)} %get-tuple-element.47.lse_ref, ...), custom_call_target="tpu_custom_call" | custom-call | tf_op jit(solution)/shard_map/pallas_call | solution.py:291
  452.0 4.5 convert_reduce_fusion
  456.5 4.4 multiply_reduce_fusion
  463.0 2.4 convert_reduce_fusion.1
  472.6 2.4 add_add_fusion.3
  476.9 2.3 add_add_fusion.2
  480.2 8.3 %fusion.9 = (f32[2048]{0:T(1024)S(1)}, f32[128]{0:T(128)S(1)}, f32[128,2048]{1,0:T(8,128)}) fusion(bf16[1,128,2048]{2,1,0:T(8,128)(2,1)S(1)} %copy-done, f32[128]{0:T(128)S(1)} %copy-done.49, f32[2048]{0:T(1024)S(1)} %bitcast.176, bf16[2048,2304]{1,0:T(8,128)(2,1)} %bitcast.134, f32[128,1536]{0,1:T(8,128)} %bitcast.148, f32[128,384]{0,1:T(8,128)} %bitcast.166, ...), kind=kOutput, calls=%fused_computation.37 | convolution fusion | flops 1210677120 | bytes 12207104 | tf_op jit(solution)/shard_map/rc,dc->rd/dot_general | solution.py:1185
  489.1 5.2 convolution_convert_fusion
  494.4 94.3 %shard_map.267 = (f32[64,2304]{1,0:T(8,128)}, bf16[64,10240]{1,0:T(8,128)(2,1)}, f32[40,128]{1,0:T(8,128)}) custom-call(bf16[2,4,2,2,64,2304]{5,4,3,2,1,0:T(8,128)(2,1)} %bitcast.135, bf16[4,2,64,1280]{3,2,1,0:T(8,128)(2,1)} %get-tuple-element.80.ge_ref, f32[40,128]{1,0:T(8,128)} %pad_select_fusion.x_ref), custom_call_target="tpu_custom_call" | custom-call | tf_op jit(solution)/shard_map/pallas_call | solution.py:291
  595.2 4.3 multiply_subtract_fusion.1
  600.0 3.0 multiply_subtract_fusion
  606.6 3.0 fusion.17
  (208 shorter events, 37.9 us)
Async XLA Ops:
  0.6 5.1 copy-start.15
  2.7 61.3 %copy-start.59 = (f32[128]{0:T(128)}, f32[128]{0:T(128)S(1)}, u32[]{:S(2)}) copy-start(f32[128]{0:T(128)S(1)} %fusion.10) | copy-start | bytes 1540
  2.7 61.3 %copy-start.48 = (f32[128]{0:T(128)}, f32[128]{0:T(128)S(1)}, u32[]{:S(2)}) copy-start(f32[128]{0:T(128)S(1)} %fusion.32) | copy-start | bytes 1540
  2.7 61.3 %copy-start = (bf16[1,128,2048]{2,1,0:T(8,128)(2,1)S(1)}, bf16[1,128,2048]{2,1,0:T(8,128)(2,1)}, u32[]{:S(2)}) copy-start(bf16[1,128,2048]{2,1,0:T(8,128)(2,1)} %param.15) | copy-start | bytes 1572868
  64.0 5.5 copy-start.56
  167.2 5.0 copy-start.6
  225.7 9.2 %copy-start.61 = (bf16[4,2,128,2048]{3,2,1,0:T(8,128)(2,1)S(1)}, bf16[4,2,128,2048]{3,2,1,0:T(8,128)(2,1)}, u32[]{:S(2)}) copy-start(bf16[4,2,128,2048]{3,2,1,0:T(8,128)(2,1)} %get-tuple-element.41) | copy-start | bytes 12582916
  225.7 9.2 %copy-start.63 = (bf16[2,2,160,2048]{3,2,1,0:T(8,128)(2,1)S(1)}, bf16[2,2,160,2048]{3,2,1,0:T(8,128)(2,1)}, u32[]{:S(2)}) copy-start(bf16[2,2,160,2048]{3,2,1,0:T(8,128)(2,1)} %get-tuple-element.43) | copy-start | bytes 7864324
  235.0 15.8 %slice-start = ((s8[5242880]{0:T(1024)(128)(4,1)}), s8[4194304]{0:T(1024)(128)(4,1)S(1)}, s32[]{:S(2)}) async-start(s8[5242880]{0:T(1024)(128)(4,1)} %bitcast.151), calls=%async_computation | async-start | bytes 8388608
  238.8 7.8 %copy-start.65 = (bf16[1024,640]{0,1:T(8,128)(2,1)}, bf16[1024,640]{0,1:T(8,128)(2,1)S(1)}, u32[]{:S(2)}) copy-start(bf16[1024,640]{0,1:T(8,128)(2,1)S(1)} %get-tuple-element.83) | copy-start | bytes 3932164
  238.8 11.9 %slice-start.1 = ((s8[5242880]{0:T(1024)(128)(4,1)}), s8[1048576]{0:T(1024)(128)(4,1)S(1)}, s32[]{:S(2)}) async-start(s8[5242880]{0:T(1024)(128)(4,1)} %bitcast.151), calls=%async_computation.1 | async-start | bytes 2097152
  312.0 4.5 copy-start.2
  312.0 4.5 copy-start.64
  312.0 4.5 copy-start.66
  456.5 4.4 copy-start.21
  463.0 5.1 copy-start.28
  463.0 5.1 copy-start.30
  463.0 6.5 %copy-start.42 = (f32[128,6]{0,1:T(8,128)S(1)}, f32[128,6]{0,1:T(8,128)}, u32[]{:S(2)}) copy-start(f32[128,6]{0,1:T(8,128)} %copy-done.41) | copy-start | bytes 9220
  463.0 6.5 %copy-start.52 = (f32[64]{0:T(128)S(1)}, f32[64]{0:T(128)}, u32[]{:S(2)}) copy-start(f32[64]{0:T(128)} %copy-done.51) | copy-start | bytes 772
  468.1 4.1 copy-start.37
  468.1 4.1 copy-start.54
  471.3 5.5 copy-start.40
  471.4 5.5 copy-start.38
  471.4 5.5 copy-start.55
  472.6 7.5 %copy-start.49 = (f32[128]{0:T(128)S(1)}, f32[128]{0:T(128)}, u32[]{:S(2)}) copy-start(f32[128]{0:T(128)} %copy-done.48) | copy-start | bytes 1540
  480.1 8.4 %copy-start.47 = (f32[2048]{0:T(1024)S(1)}, f32[2048]{0:T(1024)}, u32[]{:S(2)}) copy-start(f32[2048]{0:T(1024)} %get-tuple-element.59) | copy-start | bytes 24580
  480.2 9.0 %copy-start.4 = (f32[128,24,64]{0,2,1:T(8,128)S(1)}, f32[128,24,64]{0,2,1:T(8,128)}, u32[]{:S(2)}) copy-start(f32[128,24,64]{0,2,1:T(8,128)} %add_add_fusion.2) | copy-start | bytes 2359300
  480.2 9.0 %copy-start.17 = (f32[128,6,64]{0,2,1:T(8,128)S(1)}, f32[128,6,64]{0,2,1:T(8,128)}, u32[]{:S(2)}) copy-start(f32[128,6,64]{0,2,1:T(8,128)} %copy.80) | copy-start | bytes 589828
  480.2 9.0 %copy-start.18 = (f32[128,6,64]{0,2,1:T(8,128)S(1)}, f32[128,6,64]{0,2,1:T(8,128)}, u32[]{:S(2)}) copy-start(f32[128,6,64]{0,2,1:T(8,128)} %copy.77) | copy-start | bytes 589828
  595.2 4.3 copy-start.3
  595.2 4.3 copy-start.14
  595.2 4.8 copy-start.23
  (37 other events, 86.0 us)
